TPU v7x, 256 devices: a whole 4x4x8 slice. The times are simulated.
256 devices in a mesh: freq: 16 (over x, y_hi, core), tile: 16 (over y_lo, z).
Axes of the slice: x: 4, y: 4 (y_hi: 2, y_lo: 2; y = y_hi * 2 + y_lo), z: 8, core: 2. Of those that a mesh axis runs over, the one named last changes fastest.
Arguments:
- omega: float32 [16], P('freq'), may hold values from 0.2 to 2
- conductivity: float32 [16, 128, 256], P(None, 'tile'), may hold values from 0.1 to 10
- forward_field: float32 [16, 2, 3, 16, 128, 256], P('freq', None, None, None, 'tile'), may hold values from -6 to 6
- adjoint_start: float32 [16, 2, 3, 16, 128, 256], P('freq', None, None, None, 'tile'), may hold values from -6 to 6
- station_data: float32 [16, 2, 2, 8192], P('freq', None, None, 'tile'), may hold values from -6 to 6
- station_owner: int32 [8192, 1], P('tile'), may hold values from 0 to 15; in each aligned block of 512 rows (0 to 511, 512 to 1023, ...) at most 128 rows name the same one
- station_cell: int32 [8192], P('tile'), may hold values from 0 to 2047
Outputs:
- adjoint_field: float32 [16, 2, 3, 16, 128, 256], P('freq', None, None, None, 'tile')
- gradient: float32 [16, 128, 256], P('freq', 'tile')
Inputs may be any that keep to these rules, and one draw needn't show every extreme that they name: `station_owner`: among the 512 stations listed on one device, at most 128 have the same owner; some owner gets exactly 128 of them. `station_cell`: counted as x * 256 + y within the owner tile; several stations may share a cell.
All inputs are finite; a program needn't handle non-finite values.
Results may differ from a plain program's by a relative error of at most 0.0003.
Values sent between devices are 32-bit elements; how exact they have to be, the bound alone decides.
No kernel may reach another device: no remote copies, remote signals or barrier semaphores. Data moves between devices by JAX's collectives and lax.ppermute only.
A program may use at most 64 MiB of HBM per device.

v0:
```python
import math

import jax
import jax.numpy as jnp
from jax import lax
from jax.sharding import PartitionSpec as P

SWEEPS = 4


penalty = 0.5
damping = 0.7
diagonal_weight = 5.0
unit_steps = ((0, 1, 0), (0, 0, 1), (1, 0, 0))


def padded_2(block, sides, width):
    for axis, dim in sides:
        count = lax.axis_size(axis)
        forward = [(i, i + 1) for i in range(count - 1)]
        backward = [(target, source) for source, target in forward]
        low = lax.ppermute(
            lax.slice_in_dim(block, block.shape[dim] - width, None, axis=dim), axis, forward
        )
        high = lax.ppermute(lax.slice_in_dim(block, 0, width, axis=dim), axis, backward)
        block = jnp.concatenate([low, block, high], axis=dim)
    return block


def offset_view(padded, shift):
    depth = padded.shape[-3] - 2
    across = padded.shape[-2] - 2
    along = padded.shape[-1] - 2
    return padded[
        ...,
        1 + shift[0] : 1 + shift[0] + depth,
        1 + shift[1] : 1 + shift[1] + across,
        1 + shift[2] : 1 + shift[2] + along,
    ]


def joined(first_step, second_step, sign_one, sign_two):
    return (
        sign_one * first_step[0] + sign_two * second_step[0],
        sign_one * first_step[1] + sign_two * second_step[1],
        sign_one * first_step[2] + sign_two * second_step[2],
    )


def second_diff(field, target, source):
    step_a = unit_steps[target]
    step_b = unit_steps[source]
    if target == source:
        return (
            offset_view(field, step_a)
            - 2.0 * offset_view(field, (0, 0, 0))
            + offset_view(field, joined(step_a, step_a, -1, 0))
        )
    total = offset_view(field, joined(step_a, step_b, 1, 1)) - offset_view(
        field, joined(step_a, step_b, 1, -1)
    )
    total = (
        total
        - offset_view(field, joined(step_a, step_b, -1, 1))
        + offset_view(field, joined(step_a, step_b, -1, -1))
    )
    return total / 4.0


def relax(lam_pad, sigma, surface, omega):
    padded = jnp.pad(lam_pad, ((0, 0), (0, 0), (0, 0), (1, 1), (0, 0), (1, 1)))
    components = [padded[:, :, which] for which in range(3)]
    pieces = []
    for target in range(3):
        field = components[target]
        beside_all = jnp.zeros_like(offset_view(field, (0, 0, 0)))
        for step in unit_steps:
            beside_all = (
                beside_all
                + offset_view(field, step)
                + offset_view(field, joined(step, step, -1, 0))
            )
        value = 6.0 * offset_view(field, (0, 0, 0)) - beside_all
        bend = (
            second_diff(components[0], target, 0)
            + second_diff(components[1], target, 1)
            + second_diff(components[2], target, 2)
        )
        pieces.append(value + (1.0 - penalty) * bend)
    static = jnp.stack(pieces, axis=2)
    current = lam_pad[..., 1:-1, :]
    coupling = omega[:, None, None, None] * sigma[None]
    apply_re = static[:, 0] + coupling[:, None] * current[:, 1]
    apply_im = static[:, 1] - coupling[:, None] * current[:, 0]
    resid_re = (-apply_re).at[:, 0:2, 0].add(surface[:, 0])
    resid_im = (-apply_im).at[:, 0:2, 0].add(surface[:, 1])
    denominator = (diagonal_weight * diagonal_weight + coupling * coupling)[:, None]
    delta_re = (diagonal_weight * resid_re - coupling[:, None] * resid_im) / denominator
    delta_im = (coupling[:, None] * resid_re + diagonal_weight * resid_im) / denominator
    return current + damping * jnp.stack([delta_re, delta_im], axis=1)


def body(
    omega, conductivity, forward_field, adjoint_start, station_data, station_owner, station_cell
):
    pair_count = omega.shape[0]
    width = conductivity.shape[1]
    along = conductivity.shape[2]
    listed = station_cell.shape[0]
    my_tile = lax.axis_index("tile")
    data_rows = station_data.reshape(pair_count * 4, listed).T
    owners = station_owner[:, 0]
    got_data, got_cell, got_owner = (
        lax.all_gather(data_rows, "tile", axis=0, tiled=True),
        lax.all_gather(station_cell, "tile", axis=0, tiled=True),
        lax.all_gather(owners, "tile", axis=0, tiled=True),
    )
    valid = got_owner == my_tile
    placed = jnp.where(valid, got_cell, 0)
    values = got_data * valid[:, None].astype(jnp.float32)
    surface_flat = jnp.zeros((width * along, pair_count * 4), jnp.float32).at[placed].add(values)
    surface = surface_flat.T.reshape(pair_count, 2, 2, width, along)
    adjoint = adjoint_start
    for sweep_step in range(SWEEPS):
        edged = padded_2(adjoint, (("tile", 4),), 1)
        adjoint = relax(edged, conductivity, surface, omega)
    local_term = jnp.sum(
        omega[:, None, None, None, None]
        * (forward_field[:, 0] * adjoint[:, 1] + forward_field[:, 1] * adjoint[:, 0]),
        axis=(0, 1),
    )
    summed = lax.psum_scatter(local_term, "freq", scatter_dimension=0, tiled=True)
    pairs_all = pair_count * lax.axis_size("freq")
    gradient = summed * (1.0 / math.sqrt(pairs_all))
    return (adjoint, gradient)


def solution(mesh):
    return jax.shard_map(
        body,
        mesh=mesh,
        in_specs=(
            P("freq"),
            P(None, "tile", None),
            P("freq", None, None, None, "tile", None),
            P("freq", None, None, None, "tile", None),
            P("freq", None, None, "tile"),
            P("tile", None),
            P("tile"),
        ),
        out_specs=(P("freq", None, None, None, "tile", None), P("freq", "tile", None)),
        check_vma=False,
    )
```

profile of v0, /device:TPU:1, one launch (start us, length us, event | category | flops | bytes accessed | tf_op | source)
XLA Modules:
  0.0 337.2 jit_solution(15079208460293323368)
XLA Ops:
  7.2 1.5 fusion.155
  8.8 4.4 %collective-permute-start = (f32[1,2,3,16,1,256]{5,4,3,1,2,0:T(1,128)S(1)}, f32[1,2,3,16,1,256]{5,4,3,1,2,0:T(1,128)S(1)}, u32[]{:S(2)}, u32[]{:S(2)}) collective-permute-start(f32[1,2,3,16,1,256]{5,4,3,1,2,0:T(1,128)S(1)} %get-tuple-element.142), channel_id=1, source_target_pairs={{0,1},{1,2},{2,3},{3,4},{4,5},{5,6},{6,7},{7,8},{8,9},{9,10},{10,1... | collective-permute-start | bytes 294920 | tf_op jit(solution)/shard_map/ppermute | solution.py:22
  13.1 1.3 collective-permute-start.1
  15.1 30.0 %all-gather = s32[8192,1]{0,1:T(1,128)S(1)} all-gather(s32[512,1]{0,1:T(1,128)} %param.28), channel_id=2, replica_groups=mesh['freq'=16,'tile'=16] {'tile'}, dimensions={0}, use_global_device_ids=true | all-gather | bytes 34816 | tf_op jit(solution)/shard_map/all_gather | solution.py:116
  45.1 23.0 %all-gather.1 = s32[16,1,512]{2,1,0:T(1,128)S(1)} all-gather(s32[1,1,512]{2,1,0:T(1,128)} %bitcast.196), channel_id=1, replica_groups=mesh['freq'=16,'tile'=16] {'tile'}, dimensions={0}, use_global_device_ids=true | all-gather | bytes 34816 | tf_op jit(solution)/shard_map/all_gather | solution.py:115
  68.1 0.9 multiply_add_fusion
  70.0 58.7 %all_gather.11 = f32[8192,4]{1,0:T(8,128)} all-gather(f32[512,4]{1,0:T(8,128)S(1)} %bitcast.189), channel_id=1, replica_groups=mesh['freq'=16,'tile'=16] {'tile'}, dimensions={0}, use_global_device_ids=true | all-gather | bytes 139264 | tf_op jit(solution)/shard_map/all_gather | solution.py:114
  128.7 60.2 %scatter_custom_fusion = f32[2048,4]{1,0:T(8,128)S(1)} fusion(s32[8192]{0:T(1024)S(1)} %compare_select_fusion, f32[8192,4]{1,0:T(8,128)} %all_gather.11, f32[8192]{0:T(1024)S(1)} %convert_element_type.9, f32[]{:T(128)} %constant.217.clone.1), kind=kCustom, calls=%fused_computation.1 | custom fusion | flops 65536 | bytes 196612 | tf_op jit(solution)/shard_map/scatter-add | solution.py:121
  189.3 1.4 select_maximum_fusion.6
  194.1 2.4 collective-permute-start.2
  196.5 1.5 collective-permute-start.3
  198.1 3.7 %collective-permute-done.3 = f32[1,2,3,16,1,256]{5,4,3,1,2,0:T(1,128)S(1)} collective-permute-done((f32[1,2,3,16,1,256]{5,4,3,1,2,0:T(1,128)S(1)}, f32[1,2,3,16,1,256]{5,4,3,1,2,0:T(1,128)S(1)}, u32[]{:S(2)}, u32[]{:S(2)}) %collective-permute-start.3) | collective-permute-done | bytes 98336 | tf_op jit(solution)/shard_map/ppermute | solution.py:25
  201.9 1.4 select_maximum_fusion.4
  206.7 1.9 collective-permute-start.4
  208.6 1.3 collective-permute-start.5
  210.2 3.7 %collective-permute-done.5 = f32[1,2,3,16,1,256]{5,4,3,1,2,0:T(1,128)S(1)} collective-permute-done((f32[1,2,3,16,1,256]{5,4,3,1,2,0:T(1,128)S(1)}, f32[1,2,3,16,1,256]{5,4,3,1,2,0:T(1,128)S(1)}, u32[]{:S(2)}, u32[]{:S(2)}) %collective-permute-start.5) | collective-permute-done | bytes 98336 | tf_op jit(solution)/shard_map/ppermute | solution.py:25
  214.0 1.5 select_maximum_fusion.2
  218.8 1.9 collective-permute-start.6
  220.8 1.5 collective-permute-start.7
  222.4 3.7 %collective-permute-done.7 = f32[1,2,3,16,1,256]{5,4,3,1,2,0:T(1,128)S(1)} collective-permute-done((f32[1,2,3,16,1,256]{5,4,3,1,2,0:T(1,128)S(1)}, f32[1,2,3,16,1,256]{5,4,3,1,2,0:T(1,128)S(1)}, u32[]{:S(2)}, u32[]{:S(2)}) %collective-permute-start.7) | collective-permute-done | bytes 98336 | tf_op jit(solution)/shard_map/ppermute | solution.py:25
  226.1 1.3 select_maximum_fusion
  231.5 1.0 copy.102
  232.5 96.5 %reduce-scatter.2.cloned.1.call-done = f32[1,8,256]{2,1,0:T(8,128)} async-done(((f32[16,8,256]{2,1,0:T(8,128)}), f32[1,8,256]{2,1,0:T(8,128)}) %reduce-scatter.2.cloned.1.call-update) | async-done | bytes 8208 | tf_op jit(solution)/shard_map/reduce_scatter | solution.py:132
  329.0 1.3 broadcast_multiply_fusion.1
  (60 shorter events, 15.8 us)
Async XLA Ops:
  7.2 321.9 %reduce-scatter.2.cloned.1.call-start = ((), (), s32[]{:S(2)}) async-start(), calls=%async_computation.1 | async-start | bytes 139264 | tf_op jit(solution)/shard_map/reduce_scatter | solution.py:132
  8.8 180.5 %collective-permute-start = (f32[1,2,3,16,1,256]{5,4,3,1,2,0:T(1,128)S(1)}, f32[1,2,3,16,1,256]{5,4,3,1,2,0:T(1,128)S(1)}, u32[]{:S(2)}, u32[]{:S(2)}) collective-permute-start(f32[1,2,3,16,1,256]{5,4,3,1,2,0:T(1,128)S(1)} %get-tuple-element.142), channel_id=1, source_target_pairs={{0,1},{1,2},{2,3},{3,4},{4,5},{5,6},{6,7},{7,8},{8,9},{9,10},{10,1... | collective-permute-start | bytes 294920 | tf_op jit(solution)/shard_map/ppermute | solution.py:22
  13.1 176.1 %collective-permute-start.1 = (f32[1,2,3,16,1,256]{5,4,3,1,2,0:T(1,128)S(1)}, f32[1,2,3,16,1,256]{5,4,3,1,2,0:T(1,128)S(1)}, u32[]{:S(2)}, u32[]{:S(2)}) collective-permute-start(f32[1,2,3,16,1,256]{5,4,3,1,2,0:T(1,128)S(1)} %get-tuple-element.143), channel_id=1, source_target_pairs={{1,0},{2,1},{3,2},{4,3},{5,4},{6,5},{7,6},{8,7},{9,8},{10,9},{11,1... | collective-permute-start | bytes 294920 | tf_op jit(solution)/shard_map/ppermute | solution.py:25
  128.7 60.5 %copy-start = (f32[1,2,3,16,8,256]{5,4,3,2,1,0:T(8,128)S(1)}, f32[1,2,3,16,8,256]{5,4,3,2,1,0:T(8,128)}, u32[]{:S(2)}) copy-start(f32[1,2,3,16,8,256]{5,4,3,2,1,0:T(8,128)} %param.26) | copy-start | bytes 2359300
  193.7 4.3 %copy-start.1 = (f32[1,2,3,16,8,256]{5,4,3,2,1,0:T(8,128)S(1)}, f32[1,2,3,16,8,256]{5,4,3,2,1,0:T(8,128)}, u32[]{:S(2)}) copy-start(f32[1,2,3,16,8,256]{5,4,3,2,1,0:T(8,128)} %param.25) | copy-start | bytes 2359300
  194.1 4.1 %collective-permute-start.2 = (f32[1,2,3,16,1,256]{5,4,3,1,2,0:T(1,128)S(1)}, f32[1,2,3,16,1,256]{5,4,3,1,2,0:T(1,128)S(1)}, u32[]{:S(2)}, u32[]{:S(2)}) collective-permute-start(f32[1,2,3,16,1,256]{5,4,3,1,2,0:T(1,128)S(1)} %get-tuple-element.140), channel_id=1, source_target_pairs={{0,1},{1,2},{2,3},{3,4},{4,5},{5,6},{6,7},{7,8},{8,9},{9,10},{10,1... | collective-permute-start | bytes 294920 | tf_op jit(solution)/shard_map/ppermute | solution.py:22
  196.5 5.4 %collective-permute-start.3 = (f32[1,2,3,16,1,256]{5,4,3,1,2,0:T(1,128)S(1)}, f32[1,2,3,16,1,256]{5,4,3,1,2,0:T(1,128)S(1)}, u32[]{:S(2)}, u32[]{:S(2)}) collective-permute-start(f32[1,2,3,16,1,256]{5,4,3,1,2,0:T(1,128)S(1)} %get-tuple-element.141), channel_id=1, source_target_pairs={{1,0},{2,1},{3,2},{4,3},{5,4},{6,5},{7,6},{8,7},{9,8},{10,9},{11,1... | collective-permute-start | bytes 294920 | tf_op jit(solution)/shard_map/ppermute | solution.py:25
  206.7 3.5 %collective-permute-start.4 = (f32[1,2,3,16,1,256]{5,4,3,1,2,0:T(1,128)S(1)}, f32[1,2,3,16,1,256]{5,4,3,1,2,0:T(1,128)S(1)}, u32[]{:S(2)}, u32[]{:S(2)}) collective-permute-start(f32[1,2,3,16,1,256]{5,4,3,1,2,0:T(1,128)S(1)} %get-tuple-element.136), channel_id=1, source_target_pairs={{0,1},{1,2},{2,3},{3,4},{4,5},{5,6},{6,7},{7,8},{8,9},{9,10},{10,1... | collective-permute-start | bytes 294920 | tf_op jit(solution)/shard_map/ppermute | solution.py:22
  208.6 5.4 %collective-permute-start.5 = (f32[1,2,3,16,1,256]{5,4,3,1,2,0:T(1,128)S(1)}, f32[1,2,3,16,1,256]{5,4,3,1,2,0:T(1,128)S(1)}, u32[]{:S(2)}, u32[]{:S(2)}) collective-permute-start(f32[1,2,3,16,1,256]{5,4,3,1,2,0:T(1,128)S(1)} %get-tuple-element.137), channel_id=1, source_target_pairs={{1,0},{2,1},{3,2},{4,3},{5,4},{6,5},{7,6},{8,7},{9,8},{10,9},{11,1... | collective-permute-start | bytes 294920 | tf_op jit(solution)/shard_map/ppermute | solution.py:25
  218.8 3.6 %collective-permute-start.6 = (f32[1,2,3,16,1,256]{5,4,3,1,2,0:T(1,128)S(1)}, f32[1,2,3,16,1,256]{5,4,3,1,2,0:T(1,128)S(1)}, u32[]{:S(2)}, u32[]{:S(2)}) collective-permute-start(f32[1,2,3,16,1,256]{5,4,3,1,2,0:T(1,128)S(1)} %get-tuple-element.134), channel_id=1, source_target_pairs={{0,1},{1,2},{2,3},{3,4},{4,5},{5,6},{6,7},{7,8},{8,9},{9,10},{10,1... | collective-permute-start | bytes 294920 | tf_op jit(solution)/shard_map/ppermute | solution.py:22
  220.8 5.4 %collective-permute-start.7 = (f32[1,2,3,16,1,256]{5,4,3,1,2,0:T(1,128)S(1)}, f32[1,2,3,16,1,256]{5,4,3,1,2,0:T(1,128)S(1)}, u32[]{:S(2)}, u32[]{:S(2)}) collective-permute-start(f32[1,2,3,16,1,256]{5,4,3,1,2,0:T(1,128)S(1)} %get-tuple-element.135), channel_id=1, source_target_pairs={{1,0},{2,1},{3,2},{4,3},{5,4},{6,5},{7,6},{8,7},{9,8},{10,9},{11,1... | collective-permute-start | bytes 294920 | tf_op jit(solution)/shard_map/ppermute | solution.py:25
Sparse Core Ops, SparseCore 0:
  231.7 97.3 reduce-scatter.1
where the time goes:
time: 339 us; the launch traced here: 337 us
  blocking collectives  112 us (33%)
  waiting for transfers between devices  108 us (32%)
  other arithmetic  81.4 us (24%)
  starting transfers between devices  16.3 us (5%)
  between operations  15.2 us (4%)
  local copies, waits for them, and re-layouts  4.63 us (1%)
    reduce_scatter x1, waiting for transfers between devices, body(): lax.psum_scatter(local_term, 'freq', scatter_dimension=0, tiled=True)  96.5 us
    scatter-add x1, other arithmetic, body(): jnp.zeros((width * along, pair_count * 4), jnp.float32).at[placed]  60.2 us
    all_gather x1, blocking collectives, body(): lax.all_gather(data_rows, 'tile', axis=0, tiled=True)  58.7 us
    all_gather x1, blocking collectives, body(): lax.all_gather(owners, 'tile', axis=0, tiled=True)  30 us
    all_gather x1, blocking collectives, body(): lax.all_gather(station_cell, 'tile', axis=0, tiled=True)  23 us
    ppermute x4, waiting for transfers between devices, padded_2(): lax.ppermute(lax.slice_in_dim(block, 0, width, axis=dim), axis, backward)  11.2 us
    ppermute x4, starting transfers between devices, padded_2(): lax.ppermute(lax.slice_in_dim(block, block.shape[dim] - width, None, axis...  10.6 us
    another operation x16, other arithmetic, relax(): static = jnp.stack(pieces, axis=2)  10.5 us
  transfers between devices with their start and end apart: 9, of which 6 were waited for; matrix products, arithmetic and copies ran while one was open for 19% of the time, Pallas kernels for 0%

commit v1 on v0

v1 whole, which is shorter than its diff:
```python
import functools
import math

import jax
import jax.numpy as jnp
from jax import lax
from jax.experimental import pallas as pl
from jax.experimental.pallas import tpu as pltpu
from jax.sharding import PartitionSpec as P

SWEEPS = 4
DAMPING = 0.7
DIAGONAL = 5.0
ROWS = 8
HALF = 4
LEVELS = 16
ALONG = 256
FIELDS = 6
PLANES = FIELDS * LEVELS + LEVELS
PACKED = PLANES // 2


def pack_kernel(field_ref, sigma_ref, first_ref, last_ref):
    low = lax.broadcasted_iota(jnp.int32, (1, ROWS, ALONG), 1) < HALF
    top = FIELDS * LEVELS - PACKED
    upper = field_ref[0:PACKED]
    under = jnp.concatenate([field_ref[PACKED : PACKED + top], sigma_ref[...]], axis=0)
    first_ref[...] = jnp.where(low, upper, pltpu.roll(under, HALF, 1))
    last_ref[...] = jnp.where(low, pltpu.roll(upper, HALF, 1), under)


def surface_kernel(tile_ref, lists_ref, out_ref, acc_ref):
    start = tile_ref[0] * ROWS
    sources = lists_ref.shape[0]
    listed = lists_ref.shape[2]
    row = lax.broadcasted_iota(jnp.int32, (16, listed), 0)
    along = lax.broadcasted_iota(jnp.int32, (ALONG, listed), 0)
    acc_ref[...] = jnp.zeros_like(acc_ref)

    def step(source, carry):
        block = lists_ref[source]
        owner = block[4:5].astype(jnp.int32)
        cell = block[5:6].astype(jnp.int32)
        place = owner * ROWS + (cell >> 8) - start
        inside = (place >= -HALF) & (place < ROWS + HALF)
        place = jnp.where(inside, place & 15, 99)
        here = place == row
        high = block.astype(jnp.bfloat16).astype(jnp.float32)
        rest = block - high
        parts = []
        for which in range(4):
            for value in (high, rest):
                parts.append(
                    jnp.where(here, value[which : which + 1], 0.0).astype(jnp.bfloat16)
                )
        left = jnp.concatenate(parts, axis=0)
        right = jnp.where(along == (cell & 255), 1.0, 0.0).astype(jnp.bfloat16)
        acc_ref[...] += lax.dot_general(
            left, right, (((1,), (1,)), ((), ())), preferred_element_type=jnp.float32
        )
        return carry

    lax.fori_loop(0, sources, step, 0)
    for which in range(4):
        out_ref[which] = acc_ref[32 * which : 32 * which + 16] + acc_ref[32 * which + 16 : 32 * which + 32]


def relax_kernel(
    pairs_all,
    omega_ref,
    tile_ref,
    field_ref,
    forward_hbm,
    sigma_ref,
    below_ref,
    above_ref,
    surface_ref,
    out_ref,
    term_ref,
    one,
    two,
    coef,
    extra,
    grad,
    forward_ref,
    sem,
):
    fetch = pltpu.make_async_copy(forward_hbm, forward_ref, sem)
    fetch.start()
    sub = lax.broadcasted_iota(jnp.int32, (8, 128), 0)
    lane = lax.broadcasted_iota(jnp.int32, (8, 128), 1)
    sub_last, sub_first = sub < 7, sub > 0
    lane_last, lane_first = lane < 127, lane > 0
    low = sub < HALF
    zero = jnp.zeros((8, 128), jnp.float32)
    omega = omega_ref[0]
    tile = tile_ref[0]
    tiles = tile_ref[1]

    def load(ref, *index, rows=2):
        return [
            [ref[(*index, slice(8 * r, 8 * r + 8), slice(128 * c, 128 * c + 128))] for c in range(2)]
            for r in range(rows)
        ]

    def store(ref, value, *index):
        for r, line in enumerate(value):
            for c, piece in enumerate(line):
                ref[(*index, slice(8 * r, 8 * r + 8), slice(128 * c, 128 * c + 128))] = piece

    def both(function, *values):
        rows = min(len(v) for v in values)
        return [[function(*(v[r][c] for v in values)) for c in range(2)] for r in range(rows)]

    def x_next(value, rows=2):
        turned = [[pltpu.roll(value[r][c], 7, 0) for c in range(2)] for r in range(2)]
        return [[jnp.where(sub_last, turned[r][c], turned[1 - r][c]) for c in range(2)] for r in range(rows)]

    def x_prev(value, rows=2):
        turned = [[pltpu.roll(value[r][c], 1, 0) for c in range(2)] for r in range(2)]
        return [[jnp.where(sub_first, turned[r][c], turned[1 - r][c]) for c in range(2)] for r in range(rows)]

    def y_next(value):
        out = []
        for line in value:
            left, right = (pltpu.roll(piece, 127, 1) for piece in line)
            out.append([jnp.where(lane_last, left, right), jnp.where(lane_last, right, zero)])
        return out

    def y_prev(value):
        out = []
        for line in value:
            left, right = (pltpu.roll(piece, 1, 1) for piece in line)
            out.append([jnp.where(lane_first, left, zero), jnp.where(lane_first, right, left)])
        return out

    def plus(a, b):
        return both(lambda p, q: p + q, a, b)

    def minus(a, b):
        return both(lambda p, q: p - q, a, b)

    keep = jnp.where(low, (tile < tiles - 1).astype(jnp.int32), (tile > 0).astype(jnp.int32)) > 0

    def beside(index, upper):
        first, last = above_ref[index], below_ref[index]
        wide = lax.broadcasted_iota(jnp.int32, (8, ALONG), 0) < HALF
        if upper:
            return jnp.where(wide, first, pltpu.roll(last, HALF, 0))
        return jnp.where(wide, pltpu.roll(first, HALF, 0), last)

    blank = jnp.zeros((16, ALONG), jnp.float32)
    for buffer in (one, two):
        for field in range(FIELDS):
            buffer[field, 0] = blank
            buffer[field, LEVELS + 1] = blank
    for part in range(2):
        for edge in (0, LEVELS + 1):
            for kind in range(3):
                grad[kind, part, edge] = blank

    for field in range(FIELDS):

        def fill(level, carry, field=field):
            plane = field * LEVELS + level
            one[field, level + 1, 0:8] = field_ref[plane]
            if field * LEVELS + LEVELS <= PACKED:
                one[field, level + 1, 8:16] = beside(plane, True)
            elif field * LEVELS >= PACKED:
                one[field, level + 1, 8:16] = beside(plane - PACKED, False)
            else:

                @pl.when(plane < PACKED)
                def _():
                    one[field, level + 1, 8:16] = beside(jnp.minimum(plane, PACKED - 1), True)

                @pl.when(plane >= PACKED)
                def _():
                    one[field, level + 1, 8:16] = beside(jnp.maximum(plane - PACKED, 0), False)

            return carry

        lax.fori_loop(0, LEVELS, fill, 0)

    def weights(level, carry):
        inner = sigma_ref[level] * omega
        outer = beside(FIELDS * LEVELS - PACKED + level, False) * omega
        for r, value in enumerate((inner, outer)):
            scale = DAMPING / (DIAGONAL * DIAGONAL + value * value)
            if r == 1:
                wide = jnp.concatenate([keep, keep], axis=1)
                scale = jnp.where(wide, scale, 0.0)
            coef[0, level, 8 * r : 8 * r + 8] = DIAGONAL * scale
            coef[1, level, 8 * r : 8 * r + 8] = value * scale
        return carry

    lax.fori_loop(0, LEVELS, weights, 0)

    for comp in range(2):
        s_re, s_im = surface_ref[comp], surface_ref[2 + comp]
        extra[comp] = coef[0, 0] * s_re - coef[1, 0] * s_im
        extra[2 + comp] = coef[1, 0] * s_re + coef[0, 0] * s_im

    def prepare(source, level):
        for part in range(2):
            u = load(source, 3 * part, level + 1)
            v = load(source, 3 * part + 1, level + 1)
            up, down = x_next(u), x_prev(u)
            gx = minus(up, down)
            nx = plus(up, down)
            up, down = y_next(v), y_prev(v)
            gy = minus(up, down)
            ny = plus(up, down)
            store(grad, gx, 0, part, level + 1)
            store(grad, gy, 1, part, level + 1)
            store(grad, plus(gx, gy), 2, part, level + 1)
            store(grad, nx, 3, part, level + 1)
            store(grad, ny, 4, part, level + 1)

    def combine(own, side, mixed):
        return both(lambda p, q, m: 0.5 * p + q - 0.125 * m, own, side, mixed)

    def finish(source, target, level, last):
        rows = 1 if last else 2
        here = level + 1
        off = []
        for part in range(2):
            base = 3 * part
            u, v, w = (load(source, base + comp, here) for comp in range(3))
            gx, gy = load(grad, 0, part, here), load(grad, 1, part, here)
            wp, wm = load(source, base + 2, here + 1), load(source, base + 2, here - 1)
            gz = minus(wp, wm)
            nzw = plus(wp, wm)
            q = plus(gy, gz)
            mx = minus(x_next(q, rows), x_prev(q, rows))
            q = plus(gx, gz)[:rows]
            my = minus(y_next(q), y_prev(q))
            mz = minus(load(grad, 2, part, here + 1, rows=rows), load(grad, 2, part, here - 1, rows=rows))
            side = plus(y_next(u[:rows]), y_prev(u[:rows]))
            side = plus(side, plus(load(source, base, here + 1, rows=rows), load(source, base, here - 1, rows=rows)))
            cu = combine(load(grad, 3, part, here, rows=rows), side, mx)
            side = plus(x_next(v, rows), x_prev(v, rows))
            side = plus(
                side, plus(load(source, base + 1, here + 1, rows=rows), load(source, base + 1, here - 1, rows=rows))
            )
            cv = combine(load(grad, 4, part, here, rows=rows), side, my)
            side = plus(x_next(w, rows), x_prev(w, rows))
            side = plus(side, plus(y_next(w[:rows]), y_prev(w[:rows])))
            cw = combine(nzw[:rows], side, mz)
            off.append(((u, v, w), (cu, cv, cw)))
        c1, c2 = load(coef, 0, level, rows=rows), load(coef, 1, level, rows=rows)
        results = []
        for comp in range(3):
            re, im = off[0][0][comp][:rows], off[1][0][comp][:rows]
            cr, ci = off[0][1][comp], off[1][1][comp]
            new_re = both(lambda l, a, b, p, q: (1.0 - DAMPING) * l + (a * p - b * q), re, c1, c2, cr, ci)
            new_im = both(lambda l, a, b, p, q: (1.0 - DAMPING) * l + (b * p + a * q), im, c1, c2, cr, ci)
            results.append((new_re, new_im))
            if not last:
                store(target, new_re, comp, here)
                store(target, new_im, 3 + comp, here)
            else:
                store(out_ref, new_re, comp * LEVELS + level)
                store(out_ref, new_im, (3 + comp) * LEVELS + level)

    buffers = (one, two)
    for sweep in range(SWEEPS):
        source, target = buffers[sweep % 2], buffers[1 - sweep % 2]
        last = sweep == SWEEPS - 1
        prepare(source, 0)

        def plane(level, carry, source=source, target=target, last=last):
            prepare(source, level + 1)
            finish(source, target, level, last)
            return carry

        lax.fori_loop(0, LEVELS - 1, plane, 0)
        finish(source, target, LEVELS - 1, last)
        for part in range(2):
            for comp in range(2):
                if last:
                    index = (3 * part + comp) * LEVELS
                    out_ref[index] += extra[2 * part + comp, 0:8]
                else:
                    target[3 * part + comp, 1] += extra[2 * part + comp]

    fetch.wait()
    scale = omega * (1.0 / math.sqrt(pairs_all))

    def gather(level, carry):
        total = jnp.zeros((8, ALONG), jnp.float32)
        for comp in range(3):
            re, im = comp * LEVELS + level, (3 + comp) * LEVELS + level
            total = total + (forward_ref[re] * out_ref[im] + forward_ref[im] * out_ref[re])
        term_ref[level] = total * scale
        return carry

    lax.fori_loop(0, LEVELS, gather, 0)


def body(
    omega, conductivity, forward_field, adjoint_start, station_data, station_owner, station_cell
):
    listed = station_cell.shape[0]
    tiles = lax.axis_size("tile")
    groups = lax.axis_size("freq")
    me = lax.axis_index("tile")
    tile = jnp.stack([me, jnp.int32(tiles)]).astype(jnp.int32)
    field = adjoint_start.reshape(FIELDS * LEVELS, ROWS, ALONG)
    forward = forward_field.reshape(FIELDS * LEVELS, ROWS, ALONG)

    vmem = pl.BlockSpec(memory_space=pltpu.VMEM)
    smem = pl.BlockSpec(memory_space=pltpu.SMEM)
    f32 = jnp.float32

    lists = jnp.concatenate(
        [
            station_data.reshape(4, listed),
            station_owner.reshape(1, listed).astype(f32),
            station_cell.reshape(1, listed).astype(f32),
            jnp.zeros((2, listed), f32),
        ],
        axis=0,
    )
    sent = jnp.broadcast_to(lists[None], (tiles, 8, listed))
    got = lax.all_to_all(sent, "tile", 0, 0, tiled=True)

    first, last = pl.pallas_call(
        pack_kernel,
        out_shape=(
            jax.ShapeDtypeStruct((PACKED, ROWS, ALONG), f32),
            jax.ShapeDtypeStruct((PACKED, ROWS, ALONG), f32),
        ),
        in_specs=[vmem, vmem],
        out_specs=(vmem, vmem),
        compiler_params=pltpu.CompilerParams(vmem_limit_bytes=8 << 20),
        name="pack",
    )(field, conductivity)
    onward = [(i, i + 1) for i in range(tiles - 1)]
    back = [(i + 1, i) for i in range(tiles - 1)]
    below = lax.ppermute(last, "tile", onward)
    above = lax.ppermute(first, "tile", back)

    surface = pl.pallas_call(
        surface_kernel,
        out_shape=jax.ShapeDtypeStruct((4, 16, ALONG), f32),
        in_specs=[smem, vmem],
        out_specs=vmem,
        scratch_shapes=[pltpu.VMEM((128, ALONG), f32)],
        compiler_params=pltpu.CompilerParams(vmem_limit_bytes=8 << 20),
        name="surface",
    )(tile, got)

    adjoint, term = pl.pallas_call(
        functools.partial(relax_kernel, groups),
        out_shape=(
            jax.ShapeDtypeStruct((FIELDS * LEVELS, ROWS, ALONG), f32),
            jax.ShapeDtypeStruct((LEVELS, ROWS, ALONG), f32),
        ),
        in_specs=[smem, smem, vmem, pl.BlockSpec(memory_space=pl.ANY), vmem, vmem, vmem, vmem],
        out_specs=(vmem, vmem),
        scratch_shapes=[
            pltpu.VMEM((FIELDS, LEVELS + 2, 16, ALONG), f32),
            pltpu.VMEM((FIELDS, LEVELS + 2, 16, ALONG), f32),
            pltpu.VMEM((2, LEVELS, 16, ALONG), f32),
            pltpu.VMEM((4, 16, ALONG), f32),
            pltpu.VMEM((5, 2, LEVELS + 2, 16, ALONG), f32),
            pltpu.VMEM((FIELDS * LEVELS, ROWS, ALONG), f32),
            pltpu.SemaphoreType.DMA,
        ],
        compiler_params=pltpu.CompilerParams(vmem_limit_bytes=32 << 20),
        name="relax",
    )(omega, tile, field, forward, conductivity, below, above, surface)

    terms = lax.all_to_all(term, "freq", 0, 0, tiled=True)
    gradient = terms.reshape(groups, LEVELS // groups, ROWS, ALONG).sum(axis=0)
    return (adjoint.reshape(adjoint_start.shape), gradient)


def solution(mesh):
    return jax.shard_map(
        body,
        mesh=mesh,
        in_specs=(
            P("freq"),
            P(None, "tile", None),
            P("freq", None, None, None, "tile", None),
            P("freq", None, None, None, "tile", None),
            P("freq", None, None, "tile"),
            P("tile", None),
            P("tile"),
        ),
        out_specs=(P("freq", None, None, None, "tile", None), P("freq", "tile", None)),
        check_vma=False,
    )
```

time: 339 us -> 60.9 us (0.18)
  waiting for transfers between devices: 108 us -> 6.09 us
  blocking collectives: 112 us -> 16.6 us
  other arithmetic: 81.4 us -> 2.21 us
  Pallas kernels: 0 us -> 16.9 us
  between operations: 15.2 us -> 1.35 us
    all_gather x3 -> x0, blocking collectives: 112 us -> none  [the longest x1 58.7 us: body(): lax.all_gather(data_rows, 'tile', axis=0, tiled=True)]
    reduce_scatter x1 -> x0, waiting for transfers between devices: 96.5 us -> none  [body(): lax.psum_scatter(local_term, 'freq', scatter_dimension=0, tiled=True)]
    scatter-add x5 -> x0, other arithmetic: 60.2 us -> none  [the longest x1 60.2 us: body(): jnp.zeros((width * along, pair_count * 4), jnp.float32).at[placed]]
    pallas_call x0 -> x3, Pallas kernels: none -> 16.9 us  [the longest x1 11.8 us: body(): pl.pallas_call(functools.partial(relax_kernel, groups), out_shape=(jax.Sh...]
    all_to_all x0 -> x1, blocking collectives: none -> 16.6 us  [body(): terms = lax.all_to_all(term, 'freq', 0, 0, tiled=True)]
    ppermute x8 -> x2, starting transfers between devices: 16.2 us -> 4.57 us  [the longest x1 3.28 us: body(): below = lax.ppermute(last, 'tile', onward)]
    another operation x20 -> x1, other arithmetic: 11 us -> 0.08 us  [body(): tile = jnp.stack([me, jnp.int32(tiles)]).astype(jnp.int32)]
    all_to_all x0 -> x1, starting transfers between devices: none -> 10.3 us  [body(): got = lax.all_to_all(sent, 'tile', 0, 0, tiled=True)]
  transfers between devices with their start and end apart: 9 -> 3, of which waited for: 6 -> 3; matrix products, arithmetic and copies ran while one was open for 19% -> 0% of each run, Pallas kernels for 0% -> 8%
where the time goes in v1:
time: 60.9 us; the launch traced here: 60.3 us
  Pallas kernels  16.9 us (28%)
  blocking collectives  16.6 us (27%)
  starting transfers between devices  14.8 us (24%)
  waiting for transfers between devices  6.09 us (10%)
  local copies, waits for them, and re-layouts  2.43 us (4%)
  other arithmetic  2.21 us (4%)
  between operations  1.35 us (2%)
    all_to_all x1, blocking collectives, body(): terms = lax.all_to_all(term, 'freq', 0, 0, tiled=True)  16.6 us
    pallas_call x1, Pallas kernels, body(): pl.pallas_call(functools.partial(relax_kernel, groups), out_shape=(jax.Sh...  11.8 us
    all_to_all x1, starting transfers between devices, body(): got = lax.all_to_all(sent, 'tile', 0, 0, tiled=True)  10.3 us
    pallas_call x1, Pallas kernels, body(): pl.pallas_call(surface_kernel, out_shape=jax.ShapeDtypeStruct((4, 16, ALO...  4.26 us
    ppermute x1, starting transfers between devices, body(): below = lax.ppermute(last, 'tile', onward)  3.28 us
    ppermute x1, waiting for transfers between devices, body(): below = lax.ppermute(last, 'tile', onward)  2.77 us
    ppermute x1, waiting for transfers between devices, body(): above = lax.ppermute(first, 'tile', back)  1.66 us
    all_to_all x1, waiting for transfers between devices, body(): got = lax.all_to_all(sent, 'tile', 0, 0, tiled=True)  1.65 us
  transfers between devices with their start and end apart: 3, of which 3 were waited for; matrix products, arithmetic and copies ran while one was open for 0% of the time, Pallas kernels for 8%

profile of v1, /device:TPU:1, one launch (start us, length us, event | category | flops | bytes accessed | tf_op | source)
XLA Modules:
  0.0 60.3 jit_solution(17040291802087157467)
XLA Ops:
  0.6 0.0 copy-start
  0.6 0.8 %convert_bitcast_fusion = f32[1,512]{1,0:T(1,128)S(1)} fusion(s32[512,1]{0,1:T(1,128)} %param.12), kind=kLoop, calls=%fused_computation.1 | loop fusion | flops 512 | bytes 4096 | tf_op jit(solution)/shard_map/convert_element_type | solution.py:319
  1.4 0.7 %convert_element_type.22 = f32[512]{0:T(512)S(1)} convert(s32[512]{0:T(512)} %param.13) | non-fusion elementwise | flops 512 | bytes 4096 | tf_op jit(solution)/shard_map/convert_element_type | solution.py:320
  2.1 0.7 %reshape.37 = f32[4,512]{1,0:T(4,128)S(1)} reshape(f32[1,2,2,512]{3,2,1,0:T(2,128)} %param.11) | data formatting | bytes 16384 | tf_op jit(solution)/shard_map/reshape | solution.py:318
  2.8 0.1 pad.3.clone
  2.9 0.1 maximum_maximum_fusion
  2.9 0.7 %broadcast_in_dim.10 = f32[16,8,512]{2,1,0:T(8,128)} broadcast(f32[8,512]{1,0:T(8,128)S(1)} %maximum_maximum_fusion), dimensions={1,2} | broadcast | bytes 278528 | tf_op jit(solution)/shard_map/broadcast_in_dim | solution.py:325
  3.7 10.3 %all-to-all-start = ((f32[16,8,512]{2,1,0:T(8,128)}), f32[16,8,512]{2,1,0:T(8,128)S(1)}, u32[]{:S(2)}, u32[]{:S(2)}) async-start(f32[16,8,512]{2,1,0:T(8,128)} %broadcast_in_dim.10), calls=%async_computation | async-start | bytes 524288 | tf_op jit(solution)/shard_map/all_to_all | solution.py:326
  13.9 0.0 copy-done
  14.0 0.0 copy-start.2
  14.0 0.9 %copy-done.2 = f32[16,8,256]{2,1,0:T(8,128)S(1)} copy-done((f32[16,8,256]{2,1,0:T(8,128)S(1)}, f32[16,8,256]{2,1,0:T(8,128)}, u32[]{:S(2)}) %copy-start.2) | copy-done | bytes 131096
  14.9 0.8 %pack.1 = (f32[56,8,256]{2,1,0:T(8,128)S(1)}, f32[56,8,256]{2,1,0:T(8,128)}) custom-call(f32[96,8,256]{2,1,0:T(8,128)S(1)} %bitcast.8, f32[16,8,256]{2,1,0:T(8,128)S(1)} %copy-done.2), custom_call_target="tpu_custom_call" | custom-call | tf_op jit(solution)/shard_map/pack/pallas_call | solution.py:328
  15.7 3.3 %collective-permute-start = (f32[56,8,256]{2,1,0:T(8,128)}, f32[56,8,256]{2,1,0:T(8,128)S(1)}, u32[]{:S(2)}, u32[]{:S(2)}) collective-permute-start(f32[56,8,256]{2,1,0:T(8,128)} %get-tuple-element.6), channel_id=1, source_target_pairs={{0,1},{1,2},{2,3},{3,4},{4,5},{5,6},{6,7},{7,8},{8,9},{9,10},{10,1... | collective-permute-start | bytes 1376264 | tf_op jit(solution)/shard_map/ppermute | solution.py:341
  19.0 1.3 %collective-permute-start.1 = (f32[56,8,256]{2,1,0:T(8,128)S(1)}, f32[56,8,256]{2,1,0:T(8,128)S(1)}, u32[]{:S(2)}, u32[]{:S(2)}) collective-permute-start(f32[56,8,256]{2,1,0:T(8,128)S(1)} %get-tuple-element.7), channel_id=1, source_target_pairs={{1,0},{2,1},{3,2},{4,3},{5,4},{6,5},{7,6},{8,7},{9,8},{10,9},{11,1... | collective-permute-start | bytes 1376264 | tf_op jit(solution)/shard_map/ppermute | solution.py:342
  20.9 0.1 pad_add_fusion.tile_ref
  21.0 1.7 %all-to-all-done.lists_ref = f32[16,8,512]{2,1,0:T(8,128)S(1)} async-done(((f32[16,8,512]{2,1,0:T(8,128)}), f32[16,8,512]{2,1,0:T(8,128)S(1)}, u32[]{:S(2)}, u32[]{:S(2)}) %all-to-all-start) | async-done | bytes 262176 | tf_op jit(solution)/shard_map/all_to_all | solution.py:326
  22.7 4.3 %surface.1.surface_ref = f32[4,16,256]{2,1,0:T(8,128)S(1)} custom-call(s32[2]{0:T(128)S(1)} %pad_add_fusion.tile_ref, f32[16,8,512]{2,1,0:T(8,128)S(1)} %all-to-all-done.lists_ref), custom_call_target="tpu_custom_call" | custom-call | tf_op jit(solution)/shard_map/surface/pallas_call | solution.py:344
  26.9 2.8 %collective-permute-done.below_ref = f32[56,8,256]{2,1,0:T(8,128)S(1)} collective-permute-done((f32[56,8,256]{2,1,0:T(8,128)}, f32[56,8,256]{2,1,0:T(8,128)S(1)}, u32[]{:S(2)}, u32[]{:S(2)}) %collective-permute-start) | collective-permute-done | bytes 458784 | tf_op jit(solution)/shard_map/ppermute | solution.py:341
  29.7 1.7 %collective-permute-done.1.above_ref = f32[56,8,256]{2,1,0:T(8,128)S(1)} collective-permute-done((f32[56,8,256]{2,1,0:T(8,128)S(1)}, f32[56,8,256]{2,1,0:T(8,128)S(1)}, u32[]{:S(2)}, u32[]{:S(2)}) %collective-permute-start.1) | collective-permute-done | bytes 458784 | tf_op jit(solution)/shard_map/ppermute | solution.py:342
  31.4 0.0 copy-done.1
  31.4 0.0 copy-done.3
  31.4 11.8 %relax.1 = (f32[96,8,256]{2,1,0:T(8,128)}, f32[16,8,256]{2,1,0:T(8,128)S(1)}) custom-call(f32[1]{0:T(128)S(6)} %copy.9.omega_ref, s32[2]{0:T(128)S(1)} %pad_add_fusion.tile_ref, f32[96,8,256]{2,1,0:T(8,128)S(1)} %bitcast.9, f32[96,8,256]{2,1,0:T(8,128)S(1)} %bitcast.10, f32[16,8,256]{2,1,0:T(8,128)S(1)} %copy-done.3, ...), custom_call_target="tpu_custom_call" | custom-call | tf_op jit(solution)/shard_map/relax/pallas_call | solution.py:354
  43.2 16.6 %all_to_all.10 = f32[16,8,256]{2,1,0:T(8,128)S(1)} all-to-all(f32[16,8,256]{2,1,0:T(8,128)S(1)} %get-tuple-element.9), channel_id=1, replica_groups=mesh['freq'=16,'tile'=16] {'freq'}, dimensions={0} | all-to-all | bytes 262144 | tf_op jit(solution)/shard_map/all_to_all | solution.py:375
  59.7 0.6 %reduce_sum.11 = f32[8,256]{1,0:T(8,128)} reduce(f32[16,8,256]{2,1,0:T(8,128)S(1)} %all_to_all.10, f32[]{:T(128)} %constant.1.clone.1), dimensions={0}, to_apply=%region_0.0 | reduce | flops 30720 | bytes 139268 | tf_op jit(solution)/shard_map/reduce_sum | solution.py:376
  (3 shorter events, 0.0 us)
Async XLA Ops:
  0.6 13.3 %copy-start = (f32[1,2,3,16,8,256]{5,4,3,2,1,0:T(8,128)S(1)}, f32[1,2,3,16,8,256]{5,4,3,2,1,0:T(8,128)}, u32[]{:S(2)}) copy-start(f32[1,2,3,16,8,256]{5,4,3,2,1,0:T(8,128)} %param.10) | copy-start | bytes 2359300
  3.7 27.7 %copy-start.1 = (f32[1,2,3,16,8,256]{5,4,3,2,1,0:T(8,128)S(1)}, f32[1,2,3,16,8,256]{5,4,3,2,1,0:T(8,128)}, u32[]{:S(2)}) copy-start(f32[1,2,3,16,8,256]{5,4,3,2,1,0:T(8,128)} %param.9) | copy-start | bytes 2359300
  3.7 19.0 %all-to-all-start = ((f32[16,8,512]{2,1,0:T(8,128)}), f32[16,8,512]{2,1,0:T(8,128)S(1)}, u32[]{:S(2)}, u32[]{:S(2)}) async-start(f32[16,8,512]{2,1,0:T(8,128)} %broadcast_in_dim.10), calls=%async_computation | async-start | bytes 524288 | tf_op jit(solution)/shard_map/all_to_all | solution.py:326
  14.0 0.9 %copy-start.2 = (f32[16,8,256]{2,1,0:T(8,128)S(1)}, f32[16,8,256]{2,1,0:T(8,128)}, u32[]{:S(2)}) copy-start(f32[16,8,256]{2,1,0:T(8,128)} %sigma_ref.3) | copy-start | bytes 393220
  15.7 14.0 %collective-permute-start = (f32[56,8,256]{2,1,0:T(8,128)}, f32[56,8,256]{2,1,0:T(8,128)S(1)}, u32[]{:S(2)}, u32[]{:S(2)}) collective-permute-start(f32[56,8,256]{2,1,0:T(8,128)} %get-tuple-element.6), channel_id=1, source_target_pairs={{0,1},{1,2},{2,3},{3,4},{4,5},{5,6},{6,7},{7,8},{8,9},{9,10},{10,1... | collective-permute-start | bytes 1376264 | tf_op jit(solution)/shard_map/ppermute | solution.py:341
  19.0 12.4 %collective-permute-start.1 = (f32[56,8,256]{2,1,0:T(8,128)S(1)}, f32[56,8,256]{2,1,0:T(8,128)S(1)}, u32[]{:S(2)}, u32[]{:S(2)}) collective-permute-start(f32[56,8,256]{2,1,0:T(8,128)S(1)} %get-tuple-element.7), channel_id=1, source_target_pairs={{1,0},{2,1},{3,2},{4,3},{5,4},{6,5},{7,6},{8,7},{9,8},{10,9},{11,1... | collective-permute-start | bytes 1376264 | tf_op jit(solution)/shard_map/ppermute | solution.py:342
  21.0 10.4 %copy-start.3 = (f32[16,8,256]{2,1,0:T(8,128)S(1)}, f32[16,8,256]{2,1,0:T(8,128)}, u32[]{:S(2)}) copy-start(f32[16,8,256]{2,1,0:T(8,128)} %sigma_ref.3) | copy-start | bytes 393220

commit v2 on v0

v2 whole, which is shorter than its diff:
```python
import functools
import math

import jax
import jax.numpy as jnp
from jax import lax
from jax.experimental import pallas as pl
from jax.experimental.pallas import tpu as pltpu
from jax.sharding import PartitionSpec as P

SWEEPS = 4
DAMPING = 0.7
DIAGONAL = 5.0
ROWS = 8
HALF = 4
WIDE = 16
LEVELS = 16
ALONG = 256
FIELDS = 6
KINDS = FIELDS + 1
LINES = FIELDS * LEVELS * WIDE
HALO = HALF * KINDS * 2 * LEVELS
f32 = jnp.float32


def as_lines(planes):
    return planes.reshape(-1, ROWS, 2, 128).transpose(0, 2, 1, 3).reshape(-1, 128)


def from_lines(lines):
    return lines.reshape(-1, 2, ROWS, 128).transpose(0, 2, 1, 3).reshape(-1, ROWS, ALONG)


def pack_kernel(field_hbm, sigma_hbm, first_hbm, last_hbm, field_ref, sigma_ref, first_ref, last_ref, in_sems, out_sems):
    size = LEVELS * WIDE
    block = HALF * 2 * LEVELS
    pairs = [
        (field_hbm.at[pl.ds(kind * size, size)], field_ref.at[pl.ds(kind * size, size)])
        for kind in range(FIELDS)
    ]
    pairs.append((sigma_hbm, sigma_ref))
    copies = [
        pltpu.make_async_copy(source, target, in_sems.at[which]) for which, (source, target) in enumerate(pairs)
    ]
    for copy in copies:
        copy.start()
    sends = []
    for kind in range(KINDS):
        copies[kind].wait()
        source, base = (field_ref, kind * LEVELS) if kind < FIELDS else (sigma_ref, 0)
        for x in range(ROWS):
            target = first_ref if x < HALF else last_ref
            for side in range(2):
                for part in range(2):
                    start = (base + 8 * part) * WIDE + side * 8 + x
                    place = ((kind * HALF + x % HALF) * 2 + side) * LEVELS + 8 * part
                    target[place : place + 8] = source[pl.ds(start, 8, stride=WIDE), :]
        rows = pl.ds(kind * block, block)
        for which, (source, target) in enumerate(((first_ref, first_hbm), (last_ref, last_hbm))):
            copy = pltpu.make_async_copy(source.at[rows], target.at[rows], out_sems.at[2 * kind + which])
            copy.start()
            sends.append(copy)
    for copy in sends:
        copy.wait()


def lists_kernel(data_hbm, owner_hbm, cell_hbm, sent_hbm, data_ref, owner_ref, cell_ref, block_ref, in_sems, out_sems):
    copies = [
        pltpu.make_async_copy(source, target, in_sems.at[which])
        for which, (source, target) in enumerate(
            ((data_hbm, data_ref), (owner_hbm, owner_ref), (cell_hbm, cell_ref))
        )
    ]
    for copy in copies:
        copy.start()
    for copy in copies:
        copy.wait()
    for chunk in range(block_ref.shape[0] // 6):
        lanes = slice(128 * chunk, 128 * chunk + 128)
        row = 6 * chunk
        block_ref[row : row + 2] = data_ref[0, :, lanes]
        block_ref[row + 2 : row + 4] = data_ref[1, :, lanes]
        block_ref[row + 4 : row + 5] = owner_ref[:, lanes].astype(f32)
        block_ref[row + 5 : row + 6] = cell_ref[:, lanes].astype(f32)
    sends = [
        pltpu.make_async_copy(block_ref, sent_hbm.at[tile], out_sems.at[tile]) for tile in range(sent_hbm.shape[0])
    ]
    for copy in sends:
        copy.start()
    for copy in sends:
        copy.wait()


def surface_kernel(place_ref, lists_ref, out_ref, acc_ref):
    start = place_ref[0] * ROWS - HALF
    sources = lists_ref.shape[0]
    chunks = lists_ref.shape[1] // 6
    row = lax.broadcasted_iota(jnp.int32, (WIDE, 128), 0)
    along = lax.broadcasted_iota(jnp.int32, (ALONG, 128), 0)
    acc_ref[...] = jnp.zeros_like(acc_ref)

    def step(source, carry):
        lefts, rights = [], []
        for chunk in range(chunks):
            block = lists_ref[source, 6 * chunk : 6 * chunk + 6]
            owner = block[4:5].astype(jnp.int32)
            cell = block[5:6].astype(jnp.int32)
            here = owner * ROWS + (cell >> 8) - start == row
            high = block[0:4].astype(jnp.bfloat16).astype(f32)
            rest = block[0:4] - high
            parts = []
            for which in range(4):
                for value in (high, rest):
                    parts.append(jnp.where(here, value[which : which + 1], 0.0).astype(jnp.bfloat16))
            lefts.append(jnp.concatenate(parts, axis=0))
            rights.append(jnp.where(along == (cell & 255), 1.0, 0.0).astype(jnp.bfloat16))
        acc_ref[...] += lax.dot_general(
            jnp.concatenate(lefts, axis=1),
            jnp.concatenate(rights, axis=1),
            (((1,), (1,)), ((), ())),
            preferred_element_type=f32,
        )
        return carry

    lax.fori_loop(0, sources, step, 0)
    top = lax.broadcasted_iota(jnp.int32, (8, 128), 0) == 0
    for which in range(4):
        total = acc_ref[32 * which : 32 * which + 16] + acc_ref[32 * which + 16 : 32 * which + 32]
        for x in range(WIDE):
            for side in range(2):
                line = total[x : x + 1, 128 * side : 128 * side + 128]
                out_ref[which, x, side] = jnp.where(top, line, 0.0)


def quarters(place_ref, below_ref, above_ref):
    tile, tiles = place_ref[0], place_ref[1]
    return ((0, below_ref, tile > 0), (HALF + ROWS, above_ref, tile < tiles - 1))


def packed(ref, x, kind, side, part):
    start = ((kind * HALF + x) * 2 + side) * LEVELS + 8 * part
    return ref[pl.ds(pl.multiple_of(start, 8), 8), :]


def coef_kernel(omega_ref, place_ref, below_ref, sigma_ref, above_ref, coef):
    omega = omega_ref[0]

    def store(value, at, side, part, inside):
        value = value * omega
        scale = DAMPING / (DIAGONAL * DIAGONAL + value * value)
        if inside is not None:
            scale = jnp.where(inside, scale, 0.0)
        coef[0, at, side, 8 * part : 8 * part + 8] = DIAGONAL * scale
        coef[1, at, side, 8 * part : 8 * part + 8] = value * scale

    for base, ref, inside in quarters(place_ref, below_ref, above_ref):
        for x in range(HALF):
            for side in range(2):
                for part in range(2):
                    store(packed(ref, x, FIELDS, side, part), base + x, side, part, inside)
    for x in range(ROWS):
        for side in range(2):
            for part in range(2):
                value = sigma_ref[pl.ds(8 * part * WIDE + side * 8 + x, 8, stride=WIDE), :]
                store(value, HALF + x, side, part, None)


def relax_kernel(
    pairs_all,
    omega_ref,
    place_ref,
    below_ref,
    field_ref,
    above_ref,
    coef,
    surface_ref,
    forward_ref,
    out_ref,
    term_ref,
    one,
    two,
    total_ref,
):
    lane = lax.broadcasted_iota(jnp.int32, (8, 128), 1)
    lane_last, lane_first = lane < 127, lane > 0
    zero = jnp.zeros((8, 128), f32)
    omega = omega_ref[0]

    def clear(x, carry):
        for side in range(2):
            for field in range(FIELDS):
                for buffer in (one, two):
                    buffer[field, x, side, 0:8] = zero
                    buffer[field, x, side, 24:32] = zero
        return carry

    lax.fori_loop(0, WIDE, clear, 0)

    for base, ref, inside in quarters(place_ref, below_ref, above_ref):

        def outer(x, carry, base=base, ref=ref, inside=inside):
            for side in range(2):
                for part in range(2):
                    for field in range(FIELDS):
                        value = jnp.where(inside, packed(ref, x, field, side, part), 0.0)
                        one[field, base + x, side, 8 + 8 * part : 16 + 8 * part] = value
            return carry

        lax.fori_loop(0, HALF, outer, 0)

    def inner(x, carry):
        for side in range(2):
            for part in range(2):
                for field in range(FIELDS):
                    start = (field * LEVELS + 8 * part) * WIDE + side * 8 + x
                    value = field_ref[pl.ds(start, 8, stride=WIDE), :]
                    one[field, HALF + x, side, 8 + 8 * part : 16 + 8 * part] = value
        return carry

    lax.fori_loop(0, ROWS, inner, 0)

    def y_sum(ahead, behind):
        left, right = (pltpu.roll(piece, 127, 1) for piece in ahead)
        low, high = (pltpu.roll(piece, 1, 1) for piece in behind)
        return [
            jnp.where(lane_last, left, right) + jnp.where(lane_first, low, zero),
            jnp.where(lane_last, right, zero) + jnp.where(lane_first, high, low),
        ]

    def advance(x, source, target, last):
        for part in range(2):
            row = 8 + 8 * part
            off, old = [], []
            for half in range(2):
                ahead, behind, rest = ([], [], []), ([], [], []), ([], [], [])
                for side in range(2):

                    def at(comp, dx=0, dz=0, side=side, half=half):
                        return source[3 * half + comp, x + dx, side, row + dz : row + dz + 8]

                    u, v, w = at(0), at(1), at(2)
                    old.append((u, v, w))
                    up, down = at(0, 1), at(0, -1)
                    dxu, nxu = up - down, up + down
                    up, down = at(1, 1), at(1, -1)
                    dxv, nxv = up - down, up + down
                    up, down = at(1, 0, 1), at(1, 0, -1)
                    dzv, nzv = up - down, up + down
                    up, down = at(2, 0, 1), at(2, 0, -1)
                    dzw, nzw = up - down, up + down
                    nxw = at(2, 1) + at(2, -1)
                    nzu = at(0, 0, 1) + at(0, 0, -1)
                    ddw = (at(2, 1, 1) - at(2, 1, -1)) - (at(2, -1, 1) - at(2, -1, -1))
                    ddu = (at(0, 1, 1) - at(0, 1, -1)) - (at(0, -1, 1) - at(0, -1, -1))
                    for comp, (middle, slope) in enumerate(
                        ((u, 0.125 * dxv), (0.5 * v, 0.125 * (dxu + dzw)), (w, 0.125 * dzv))
                    ):
                        ahead[comp].append(middle - slope)
                        behind[comp].append(middle + slope)
                    rest[0].append((0.5 * nxu + nzu) - 0.125 * ddw)
                    rest[1].append(nxv + nzv)
                    rest[2].append((0.5 * nzw + nxw) - 0.125 * ddu)
                for comp in range(3):
                    sums = y_sum(ahead[comp], behind[comp])
                    value = [rest[comp][side] + sums[side] for side in range(2)]
                    if part == 0 and comp < 2:
                        value = [value[side] + surface_ref[2 * half + comp, x, side] for side in range(2)]
                    off.append(value)
            for side in range(2):
                c1 = coef[0, x, side, 8 * part : 8 * part + 8]
                c2 = coef[1, x, side, 8 * part : 8 * part + 8]
                total = None
                for comp in range(3):
                    re, im = off[comp][side], off[3 + comp][side]
                    new_re = (1.0 - DAMPING) * old[side][comp] + (c1 * re - c2 * im)
                    new_im = (1.0 - DAMPING) * old[2 + side][comp] + (c2 * re + c1 * im)
                    if not last:
                        target[comp, x, side, row : row + 8] = new_re
                        target[3 + comp, x, side, row : row + 8] = new_im
                    else:
                        base = side * 8 + x - HALF
                        re_at = pl.ds((comp * LEVELS + 8 * part) * WIDE + base, 8, stride=WIDE)
                        im_at = pl.ds(((3 + comp) * LEVELS + 8 * part) * WIDE + base, 8, stride=WIDE)
                        out_ref[re_at, :] = new_re
                        out_ref[im_at, :] = new_im
                        piece = forward_ref[re_at, :] * new_im + forward_ref[im_at, :] * new_re
                        total = piece if total is None else total + piece
                if last:
                    total_ref[pl.ds(8 * part * WIDE + side * 8 + x - HALF, 8, stride=WIDE), :] = total

    buffers = (one, two)
    for sweep in range(SWEEPS):
        source, target = buffers[sweep % 2], buffers[1 - sweep % 2]
        last = sweep == SWEEPS - 1

        def slice_of(step, carry, source=source, target=target, last=last, begin=1 + sweep):
            for x in range(2):
                advance(begin + 2 * step + x, source, target, last)
            return carry

        lax.fori_loop(0, (WIDE - 2 - 2 * sweep) // 2, slice_of, 0)

    scale = omega * (1.0 / math.sqrt(pairs_all))
    term_ref[...] = total_ref[...] * scale


def body(
    omega, conductivity, forward_field, adjoint_start, station_data, station_owner, station_cell
):
    listed = station_cell.shape[0]
    tiles = lax.axis_size("tile")
    groups = lax.axis_size("freq")
    place = jnp.stack([lax.axis_index("tile"), jnp.int32(tiles)])

    vmem = pl.BlockSpec(memory_space=pltpu.VMEM)
    smem = pl.BlockSpec(memory_space=pltpu.SMEM)

    far = pl.BlockSpec(memory_space=pltpu.HBM)
    sent = pl.pallas_call(
        lists_kernel,
        out_shape=jax.ShapeDtypeStruct((tiles, 6 * listed // 128, 128), f32),
        in_specs=[far] * 3,
        out_specs=far,
        scratch_shapes=[
            pltpu.VMEM((2, 2, listed), f32),
            pltpu.VMEM((1, listed), jnp.int32),
            pltpu.VMEM((1, listed), jnp.int32),
            pltpu.VMEM((6 * listed // 128, 128), f32),
            pltpu.SemaphoreType.DMA((3,)),
            pltpu.SemaphoreType.DMA((tiles,)),
        ],
        name="lists",
    )(station_data.reshape(2, 2, listed), station_owner.reshape(1, listed), station_cell.reshape(1, listed))
    first, last = pl.pallas_call(
        pack_kernel,
        out_shape=(
            jax.ShapeDtypeStruct((HALO, 128), f32),
            jax.ShapeDtypeStruct((HALO, 128), f32),
        ),
        in_specs=[far] * 2,
        out_specs=(far, far),
        scratch_shapes=[
            pltpu.VMEM((LINES, 128), f32),
            pltpu.VMEM((LEVELS * WIDE, 128), f32),
            pltpu.VMEM((HALO, 128), f32),
            pltpu.VMEM((HALO, 128), f32),
            pltpu.SemaphoreType.DMA((KINDS,)),
            pltpu.SemaphoreType.DMA((2 * KINDS,)),
        ],
        name="pack",
    )(as_lines(adjoint_start), as_lines(conductivity))
    below = lax.ppermute(last, "tile", [(i, (i + 1) % tiles) for i in range(tiles)])
    above = lax.ppermute(first, "tile", [((i + 1) % tiles, i) for i in range(tiles)])
    got = lax.all_to_all(sent, "tile", 0, 0, tiled=True)

    surface = pl.pallas_call(
        surface_kernel,
        out_shape=jax.ShapeDtypeStruct((4, WIDE, 2, 8, 128), f32),
        in_specs=[smem, vmem],
        out_specs=vmem,
        scratch_shapes=[pltpu.VMEM((128, ALONG), f32)],
        compiler_params=pltpu.CompilerParams(vmem_limit_bytes=4 << 20),
        cost_estimate=pl.CostEstimate(flops=10**9, bytes_accessed=10**6, transcendentals=0),
        name="surface",
    )(place, got)

    coef = pl.pallas_call(
        coef_kernel,
        out_shape=jax.ShapeDtypeStruct((2, WIDE, 2, LEVELS, 128), f32),
        in_specs=[smem, smem] + [vmem] * 3,
        out_specs=vmem,
        compiler_params=pltpu.CompilerParams(vmem_limit_bytes=4 << 20),
        name="coef",
    )(omega, place, below, as_lines(conductivity), above)

    adjoint, term = pl.pallas_call(
        functools.partial(relax_kernel, groups),
        out_shape=(
            jax.ShapeDtypeStruct((LINES, 128), f32),
            jax.ShapeDtypeStruct((LEVELS * WIDE, 128), f32),
        ),
        in_specs=[smem, smem] + [vmem] * 6,
        out_specs=(vmem, vmem),
        scratch_shapes=[
            pltpu.VMEM((FIELDS, WIDE, 2, 32, 128), f32),
            pltpu.VMEM((FIELDS, WIDE, 2, 32, 128), f32),
            pltpu.VMEM((LEVELS * WIDE, 128), f32),
        ],
        compiler_params=pltpu.CompilerParams(vmem_limit_bytes=12 << 20),
        name="relax",
    )(omega, place, below, as_lines(adjoint_start), above, coef, surface, as_lines(forward_field))

    terms = lax.all_to_all(term.reshape(groups, -1, 128), "freq", 0, 0, tiled=True)
    gradient = from_lines(terms.sum(axis=0))
    return (from_lines(adjoint).reshape(adjoint_start.shape), gradient)


def solution(mesh):
    return jax.shard_map(
        body,
        mesh=mesh,
        in_specs=(
            P("freq"),
            P(None, "tile", None),
            P("freq", None, None, None, "tile", None),
            P("freq", None, None, None, "tile", None),
            P("freq", None, None, "tile"),
            P("tile", None),
            P("tile"),
        ),
        out_specs=(P("freq", None, None, None, "tile", None), P("freq", "tile", None)),
        check_vma=False,
    )
```

time: 339 us -> 55.3 us (0.16)
  waiting for transfers between devices: 108 us -> 7.91 us
  blocking collectives: 112 us -> 15 us
  other arithmetic: 81.4 us -> 0.69 us
  Pallas kernels: 0 us -> 16.2 us
  between operations: 15.2 us -> 1.36 us
  local copies, waits for them, and re-layouts: 4.63 us -> 0.02 us
    all_gather x3 -> x0, blocking collectives: 112 us -> none  [the longest x1 58.7 us: body(): lax.all_gather(data_rows, 'tile', axis=0, tiled=True)]
    reduce_scatter x1 -> x0, waiting for transfers between devices: 96.5 us -> none  [body(): lax.psum_scatter(local_term, 'freq', scatter_dimension=0, tiled=True)]
    scatter-add x5 -> x0, other arithmetic: 60.2 us -> none  [the longest x1 60.2 us: body(): jnp.zeros((width * along, pair_count * 4), jnp.float32).at[placed]]
    pallas_call x0 -> x5, Pallas kernels: none -> 16.2 us  [the longest x1 7.61 us: body(): pl.pallas_call(functools.partial(relax_kernel, groups), out_shape=(jax.Sh...]
    all_to_all x0 -> x1, blocking collectives: none -> 15 us  [body(): lax.all_to_all(term.reshape(groups, -1, 128), 'freq', 0, 0, tiled=True)]
    ppermute x8 -> x2, starting transfers between devices: 16.2 us -> 3.65 us  [the longest x1 2.22 us: body(): lax.ppermute(first, 'tile', [((i + 1) % tiles, i) for i in range(tiles)])]
    another operation x20 -> x1, other arithmetic: 11 us -> 0.08 us  [body(): place = jnp.stack([lax.axis_index('tile'), jnp.int32(tiles)])]
    all_to_all x0 -> x1, starting transfers between devices: none -> 10.1 us  [body(): got = lax.all_to_all(sent, 'tile', 0, 0, tiled=True)]
  transfers between devices with their start and end apart: 9 -> 3, of which waited for: 6 -> 2; matrix products, arithmetic and copies ran while one was open for 19% -> 0% of each run, Pallas kernels for 0% -> 12%
where the time goes in v2:
time: 55.3 us; the launch traced here: 55 us
  Pallas kernels  16.2 us (29%)
  blocking collectives  15 us (27%)
  starting transfers between devices  13.8 us (25%)
  waiting for transfers between devices  7.91 us (14%)
  between operations  1.36 us (2%)
  other arithmetic  0.69 us (1%)
    all_to_all x1, blocking collectives, body(): lax.all_to_all(term.reshape(groups, -1, 128), 'freq', 0, 0, tiled=True)  15 us
    all_to_all x1, starting transfers between devices, body(): got = lax.all_to_all(sent, 'tile', 0, 0, tiled=True)  10.1 us
    pallas_call x1, Pallas kernels, body(): pl.pallas_call(functools.partial(relax_kernel, groups), out_shape=(jax.Sh...  7.61 us
    ppermute x1, waiting for transfers between devices, body(): lax.ppermute(last, 'tile', [(i, (i + 1) % tiles) for i in range(tiles)])  6.89 us
    pallas_call x1, Pallas kernels, body(): pl.pallas_call(surface_kernel, out_shape=jax.ShapeDtypeStruct((4, WIDE, 2...  4.3 us
    ppermute x1, starting transfers between devices, body(): lax.ppermute(first, 'tile', [((i + 1) % tiles, i) for i in range(tiles)])  2.22 us
    pallas_call x1, Pallas kernels, body(): pl.pallas_call(pack_kernel, out_shape=(jax.ShapeDtypeStruct((HALO, 128),...  2.11 us
    pallas_call x1, Pallas kernels, body(): pl.pallas_call(lists_kernel, out_shape=jax.ShapeDtypeStruct((tiles, 6 * l...  1.57 us
  transfers between devices with their start and end apart: 3, of which 2 were waited for; matrix products, arithmetic and copies ran while one was open for 0% of the time, Pallas kernels for 12%

profile of v2, /device:TPU:1, one launch (start us, length us, event | category | flops | bytes accessed | tf_op | source)
XLA Modules:
  0.0 55.0 jit_solution(15879762065848824169)
XLA Ops:
  0.6 1.6 %lists.1 = f32[16,24,128]{2,1,0:T(8,128)} custom-call(f32[2,2,512]{2,1,0:T(2,128)} %bitcast.36, s32[1,512]{1,0:T(1,128)} %bitcast.38, s32[1,512]{1,0:T(1,128)} %bitcast.39), custom_call_target="tpu_custom_call" | custom-call | tf_op jit(solution)/shard_map/lists/pallas_call | solution.py:319
  2.2 10.1 %all-to-all-start = ((f32[16,24,128]{2,1,0:T(8,128)}), f32[16,24,128]{2,1,0:T(8,128)S(1)}, u32[]{:S(2)}, u32[]{:S(2)}) async-start(f32[16,24,128]{2,1,0:T(8,128)} %lists.1), calls=%async_computation | async-start | bytes 393216 | tf_op jit(solution)/shard_map/all_to_all | solution.py:354
  12.4 2.1 %pack.1 = (f32[896,128]{1,0:T(8,128)}, f32[896,128]{1,0:T(8,128)}) custom-call(f32[1536,128]{1,0:T(8,128)} %bitcast.30, f32[256,128]{1,0:T(8,128)} %bitcast.33), custom_call_target="tpu_custom_call" | custom-call | tf_op jit(solution)/shard_map/pack/pallas_call | solution.py:334
  14.5 1.4 %collective-permute-start = (f32[896,128]{1,0:T(8,128)}, f32[896,128]{1,0:T(8,128)S(1)}, u32[]{:S(2)}, u32[]{:S(2)}) collective-permute-start(f32[896,128]{1,0:T(8,128)} %get-tuple-element.6), channel_id=1, source_target_pairs={{0,1},{1,2},{2,3},{3,4},{4,5},{5,6},{6,7},{7,8},{8,9},{9,10},{10,1... | collective-permute-start | bytes 1376264 | tf_op jit(solution)/shard_map/ppermute | solution.py:352
  15.9 2.2 %collective-permute-start.1 = (f32[896,128]{1,0:T(8,128)}, f32[896,128]{1,0:T(8,128)S(1)}, u32[]{:S(2)}, u32[]{:S(2)}) collective-permute-start(f32[896,128]{1,0:T(8,128)} %get-tuple-element.7), channel_id=1, source_target_pairs={{1,0},{2,1},{3,2},{4,3},{5,4},{6,5},{7,6},{8,7},{9,8},{10,9},{11,1... | collective-permute-start | bytes 1376264 | tf_op jit(solution)/shard_map/ppermute | solution.py:353
  18.8 0.1 pad_add_fusion.place_ref
  18.9 0.0 copy-start.2
  18.9 1.0 %all-to-all-done.lists_ref = f32[16,24,128]{2,1,0:T(8,128)S(1)} async-done(((f32[16,24,128]{2,1,0:T(8,128)}), f32[16,24,128]{2,1,0:T(8,128)S(1)}, u32[]{:S(2)}, u32[]{:S(2)}) %all-to-all-start) | async-done | bytes 196640 | tf_op jit(solution)/shard_map/all_to_all | solution.py:354
  19.9 4.3 %surface.1.surface_ref = f32[4,16,2,8,128]{4,3,2,1,0:T(8,128)S(1)} custom-call(s32[2]{0:T(128)S(1)} %pad_add_fusion.place_ref, f32[16,24,128]{2,1,0:T(8,128)S(1)} %all-to-all-done.lists_ref), custom_call_target="tpu_custom_call" | custom-call | flops 1000000000 | bytes 1000000 | tf_op jit(solution)/shard_map/surface/pallas_call | solution.py:356
  24.2 0.0 copy-start
  24.2 0.0 copy-start.1
  24.2 6.9 %collective-permute-done.below_ref = f32[896,128]{1,0:T(8,128)S(1)} collective-permute-done((f32[896,128]{1,0:T(8,128)}, f32[896,128]{1,0:T(8,128)S(1)}, u32[]{:S(2)}, u32[]{:S(2)}) %collective-permute-start) | collective-permute-done | bytes 458784 | tf_op jit(solution)/shard_map/ppermute | solution.py:352
  31.1 0.0 collective-permute-done.1.above_ref
  31.1 0.0 copy-done.2
  31.1 0.6 %coef.1 = f32[2,16,2,16,128]{4,3,2,1,0:T(8,128)S(1)} custom-call(f32[1]{0:T(128)S(6)} %copy.9.omega_ref, s32[2]{0:T(128)S(1)} %pad_add_fusion.place_ref, f32[896,128]{1,0:T(8,128)S(1)} %collective-permute-done.below_ref, f32[256,128]{1,0:T(8,128)S(1)} %bitcast.34, f32[896,128]{1,0:T(8,128)S(1)} %collective-permute-done.1.above_ref), custom_call_target="tpu_custom_call" | custom-call | tf_op jit(solution)/shard_map/coef/pallas_call | solution.py:367
  31.8 0.0 copy-done
  31.8 0.0 copy-done.1
  31.8 7.6 %relax.1 = (f32[1536,128]{1,0:T(8,128)}, f32[256,128]{1,0:T(8,128)S(1)}) custom-call(f32[1]{0:T(128)S(6)} %copy.9.omega_ref, s32[2]{0:T(128)S(1)} %pad_add_fusion.place_ref, f32[896,128]{1,0:T(8,128)S(1)} %collective-permute-done.below_ref, f32[1536,128]{1,0:T(8,128)S(1)} %bitcast.31, f32[896,128]{1,0:T(8,128)S(1)} %collective-permute-done.1.above_ref, ...), custom_call_target="tpu_custom_call" | custom-call | tf_op jit(solution)/shard_map/relax/pallas_call | solution.py:376
  39.4 15.0 %all_to_all.10 = f32[16,16,128]{2,1,0:T(8,128)S(1)} all-to-all(f32[16,16,128]{2,1,0:T(8,128)S(1)} %bitcast.35), channel_id=1, replica_groups=mesh['freq'=16,'tile'=16] {'freq'}, dimensions={0} | all-to-all | bytes 262144 | tf_op jit(solution)/shard_map/all_to_all | solution.py:393
  54.3 0.6 %reduce_sum.9 = f32[16,128]{1,0:T(8,128)} reduce(f32[16,16,128]{2,1,0:T(8,128)S(1)} %all_to_all.10, f32[]{:T(128)} %constant.2.clone.1), dimensions={0}, to_apply=%region_0.0 | reduce | flops 30720 | bytes 139268 | tf_op jit(solution)/shard_map/reduce_sum | solution.py:394
Async XLA Ops:
  2.2 17.7 %all-to-all-start = ((f32[16,24,128]{2,1,0:T(8,128)}), f32[16,24,128]{2,1,0:T(8,128)S(1)}, u32[]{:S(2)}, u32[]{:S(2)}) async-start(f32[16,24,128]{2,1,0:T(8,128)} %lists.1), calls=%async_computation | async-start | bytes 393216 | tf_op jit(solution)/shard_map/all_to_all | solution.py:354
  14.5 16.6 %collective-permute-start = (f32[896,128]{1,0:T(8,128)}, f32[896,128]{1,0:T(8,128)S(1)}, u32[]{:S(2)}, u32[]{:S(2)}) collective-permute-start(f32[896,128]{1,0:T(8,128)} %get-tuple-element.6), channel_id=1, source_target_pairs={{0,1},{1,2},{2,3},{3,4},{4,5},{5,6},{6,7},{7,8},{8,9},{9,10},{10,1... | collective-permute-start | bytes 1376264 | tf_op jit(solution)/shard_map/ppermute | solution.py:352
  15.9 15.2 %collective-permute-start.1 = (f32[896,128]{1,0:T(8,128)}, f32[896,128]{1,0:T(8,128)S(1)}, u32[]{:S(2)}, u32[]{:S(2)}) collective-permute-start(f32[896,128]{1,0:T(8,128)} %get-tuple-element.7), channel_id=1, source_target_pairs={{1,0},{2,1},{3,2},{4,3},{5,4},{6,5},{7,6},{8,7},{9,8},{10,9},{11,1... | collective-permute-start | bytes 1376264 | tf_op jit(solution)/shard_map/ppermute | solution.py:353
  18.9 12.3 %copy-start.2 = (f32[16,8,256]{2,1,0:T(8,128)S(1)}, f32[16,8,256]{2,1,0:T(8,128)}, u32[]{:S(2)}) copy-start(f32[16,8,256]{2,1,0:T(8,128)} %param.8) | copy-start | bytes 393220
  24.2 7.6 %copy-start = (f32[1,2,3,16,8,256]{5,4,3,2,1,0:T(8,128)S(1)}, f32[1,2,3,16,8,256]{5,4,3,2,1,0:T(8,128)}, u32[]{:S(2)}) copy-start(f32[1,2,3,16,8,256]{5,4,3,2,1,0:T(8,128)} %param.10) | copy-start | bytes 2359300
  24.2 7.6 %copy-start.1 = (f32[1,2,3,16,8,256]{5,4,3,2,1,0:T(8,128)S(1)}, f32[1,2,3,16,8,256]{5,4,3,2,1,0:T(8,128)}, u32[]{:S(2)}) copy-start(f32[1,2,3,16,8,256]{5,4,3,2,1,0:T(8,128)} %param.9) | copy-start | bytes 2359300

commit v3 on v2

v3 whole, which is shorter than its diff:
```python
import functools
import math

import jax
import jax.numpy as jnp
from jax import lax
from jax.experimental import pallas as pl
from jax.experimental.pallas import tpu as pltpu
from jax.sharding import PartitionSpec as P

SWEEPS = 4
DAMPING = 0.7
DIAGONAL = 5.0
ROWS = 8
HALF = 4
WIDE = 16
LEVELS = 16
ALONG = 256
FIELDS = 6
KINDS = FIELDS + 1
LINES = FIELDS * LEVELS * WIDE
HALO = HALF * KINDS * 2 * LEVELS
f32 = jnp.float32


def as_lines(planes):
    return planes.reshape(-1, ROWS, 2, 128).transpose(0, 2, 1, 3).reshape(-1, 128)


def from_lines(lines):
    return lines.reshape(-1, 2, ROWS, 128).transpose(0, 2, 1, 3).reshape(-1, ROWS, ALONG)


def pack_kernel(field_ref, sigma_ref, first_ref, last_ref):
    for kind in range(KINDS):
        source, base = (field_ref, kind * LEVELS) if kind < FIELDS else (sigma_ref, 0)
        for x in range(ROWS):
            target = first_ref if x < HALF else last_ref
            for side in range(2):
                for part in range(2):
                    start = (base + 8 * part) * WIDE + side * 8 + x
                    place = ((kind * HALF + x % HALF) * 2 + side) * LEVELS + 8 * part
                    target[place : place + 8] = source[pl.ds(start, 8, stride=WIDE), :]


def lists_kernel(data_hbm, owner_hbm, cell_hbm, sent_hbm, data_ref, owner_ref, cell_ref, block_ref, in_sems, out_sems):
    copies = [
        pltpu.make_async_copy(source, target, in_sems.at[which])
        for which, (source, target) in enumerate(
            ((data_hbm, data_ref), (owner_hbm, owner_ref), (cell_hbm, cell_ref))
        )
    ]
    for copy in copies:
        copy.start()
    for copy in copies:
        copy.wait()
    for chunk in range(block_ref.shape[0] // 6):
        lanes = slice(128 * chunk, 128 * chunk + 128)
        row = 6 * chunk
        block_ref[row : row + 2] = data_ref[0, :, lanes]
        block_ref[row + 2 : row + 4] = data_ref[1, :, lanes]
        block_ref[row + 4 : row + 5] = owner_ref[:, lanes].astype(f32)
        block_ref[row + 5 : row + 6] = cell_ref[:, lanes].astype(f32)
    sends = [
        pltpu.make_async_copy(block_ref, sent_hbm.at[tile], out_sems.at[tile]) for tile in range(sent_hbm.shape[0])
    ]
    for copy in sends:
        copy.start()
    for copy in sends:
        copy.wait()


def store_kernel(value_ref, out_hbm, sems):
    count = sems.shape[0]
    size = value_ref.shape[0] // count
    copies = [
        pltpu.make_async_copy(
            value_ref.at[pl.ds(size * which, size)], out_hbm.at[pl.ds(size * which, size)], sems.at[which]
        )
        for which in range(count)
    ]
    for copy in copies:
        copy.start()
    for copy in copies:
        copy.wait()


def quarters(place_ref, below_ref, above_ref):
    tile, tiles = place_ref[0], place_ref[1]
    return ((0, below_ref, tile > 0), (HALF + ROWS, above_ref, tile < tiles - 1))


def packed(ref, x, kind, side, part):
    start = ((kind * HALF + x) * 2 + side) * LEVELS + 8 * part
    return ref[pl.ds(pl.multiple_of(start, 8), 8), :]


def set_weights(coef, omega, value, at, side, part, inside=None):
    value = value * omega
    scale = DAMPING / (DIAGONAL * DIAGONAL + value * value)
    if inside is not None:
        scale = jnp.where(inside, scale, 0.0)
    coef[0, at, side, 8 * part : 8 * part + 8] = DIAGONAL * scale
    coef[1, at, side, 8 * part : 8 * part + 8] = value * scale


def y_sum(ahead, behind):
    lane = lax.broadcasted_iota(jnp.int32, (8, 128), 1)
    lane_last, lane_first = lane < 127, lane > 0
    left, right = (pltpu.roll(piece, 127, 1) for piece in ahead)
    low, high = (pltpu.roll(piece, 1, 1) for piece in behind)
    return [
        jnp.where(lane_last, left, right) + jnp.where(lane_first, low, 0.0),
        jnp.where(lane_last, right, 0.0) + jnp.where(lane_first, high, low),
    ]


def advance(x, source, coef, surface_ref, emit):
    for part in range(2):
        row = 8 + 8 * part
        off, old = [], []
        for half in range(2):
            ahead, behind, rest = ([], [], []), ([], [], []), ([], [], [])
            for side in range(2):

                def at(comp, dx=0, dz=0, side=side, half=half):
                    return source[3 * half + comp, x + dx, side, row + dz : row + dz + 8]

                u, v, w = at(0), at(1), at(2)
                old.append((u, v, w))
                up, down = at(0, 1), at(0, -1)
                dxu, nxu = up - down, up + down
                up, down = at(1, 1), at(1, -1)
                dxv, nxv = up - down, up + down
                up, down = at(1, 0, 1), at(1, 0, -1)
                dzv, nzv = up - down, up + down
                up, down = at(2, 0, 1), at(2, 0, -1)
                dzw, nzw = up - down, up + down
                nxw = at(2, 1) + at(2, -1)
                nzu = at(0, 0, 1) + at(0, 0, -1)
                ddw = (at(2, 1, 1) - at(2, 1, -1)) - (at(2, -1, 1) - at(2, -1, -1))
                ddu = (at(0, 1, 1) - at(0, 1, -1)) - (at(0, -1, 1) - at(0, -1, -1))
                for comp, (middle, slope) in enumerate(
                    ((u, 0.125 * dxv), (0.5 * v, 0.125 * (dxu + dzw)), (w, 0.125 * dzv))
                ):
                    ahead[comp].append(middle - slope)
                    behind[comp].append(middle + slope)
                rest[0].append((0.5 * nxu + nzu) - 0.125 * ddw)
                rest[1].append(nxv + nzv)
                rest[2].append((0.5 * nzw + nxw) - 0.125 * ddu)
            for comp in range(3):
                sums = y_sum(ahead[comp], behind[comp])
                value = [rest[comp][side] + sums[side] for side in range(2)]
                if part == 0 and comp < 2:
                    value = [value[side] + surface_ref[2 * half + comp, x, side] for side in range(2)]
                off.append(value)
        for side in range(2):
            c1 = coef[0, x, side, 8 * part : 8 * part + 8]
            c2 = coef[1, x, side, 8 * part : 8 * part + 8]
            news = []
            for comp in range(3):
                re, im = off[comp][side], off[3 + comp][side]
                new_re = (1.0 - DAMPING) * old[side][comp] + (c1 * re - c2 * im)
                new_im = (1.0 - DAMPING) * old[2 + side][comp] + (c2 * re + c1 * im)
                news.append((new_re, new_im))
            emit(x, side, part, news)


def keep_in(target):
    def emit(x, side, part, news):
        for comp, (new_re, new_im) in enumerate(news):
            target[comp, x, side, 8 + 8 * part : 16 + 8 * part] = new_re
            target[3 + comp, x, side, 8 + 8 * part : 16 + 8 * part] = new_im

    return emit


def surface_kernel(place_ref, lists_ref, out_ref, acc_ref):
    start = place_ref[0] * ROWS - HALF
    sources = lists_ref.shape[0]
    chunks = lists_ref.shape[1] // 6
    row = lax.broadcasted_iota(jnp.int32, (WIDE, 128), 0)
    along = lax.broadcasted_iota(jnp.int32, (ALONG, 128), 0)
    acc_ref[...] = jnp.zeros_like(acc_ref)

    def step(source, carry):
        lefts, rights = [], []
        for chunk in range(chunks):
            block = lists_ref[source, 6 * chunk : 6 * chunk + 6]
            owner = block[4:5].astype(jnp.int32)
            cell = block[5:6].astype(jnp.int32)
            here = owner * ROWS + (cell >> 8) - start == row
            high = block[0:4].astype(jnp.bfloat16).astype(f32)
            rest = block[0:4] - high
            parts = []
            for which in range(4):
                for value in (high, rest):
                    parts.append(jnp.where(here, value[which : which + 1], 0.0).astype(jnp.bfloat16))
            lefts.append(jnp.concatenate(parts, axis=0))
            rights.append(jnp.where(along == (cell & 255), 1.0, 0.0).astype(jnp.bfloat16))
        acc_ref[...] += lax.dot_general(
            jnp.concatenate(lefts, axis=1),
            jnp.concatenate(rights, axis=1),
            (((1,), (1,)), ((), ())),
            preferred_element_type=f32,
        )
        return carry

    lax.fori_loop(0, sources, step, 0)
    top = lax.broadcasted_iota(jnp.int32, (8, 128), 0) == 0
    for which in range(4):
        total = acc_ref[32 * which : 32 * which + 16] + acc_ref[32 * which + 16 : 32 * which + 32]
        for x in range(WIDE):
            for side in range(2):
                line = total[x : x + 1, 128 * side : 128 * side + 128]
                out_ref[which, x, side] = jnp.where(top, line, 0.0)


def inner_kernel(omega_ref, field_ref, sigma_ref, surface_ref, one, two, coef):
    omega = omega_ref[0]
    zero = jnp.zeros((8, 128), f32)

    def clear(x, carry):
        for side in range(2):
            for field in range(FIELDS):
                for buffer in (one, two):
                    buffer[field, x, side, 0:8] = zero
                    buffer[field, x, side, 24:32] = zero
        return carry

    lax.fori_loop(0, WIDE, clear, 0)

    def fill(x, carry):
        for side in range(2):
            for part in range(2):
                for field in range(FIELDS):
                    at = (field * LEVELS + 8 * part) * WIDE + side * 8 + x
                    value = field_ref[pl.ds(at, 8, stride=WIDE), :]
                    one[field, HALF + x, side, 8 + 8 * part : 16 + 8 * part] = value
                value = sigma_ref[pl.ds(8 * part * WIDE + side * 8 + x, 8, stride=WIDE), :]
                set_weights(coef, omega, value, HALF + x, side, part)
        return carry

    lax.fori_loop(0, ROWS, fill, 0)

    buffers = (one, two)
    for sweep in range(SWEEPS - 1):
        source, target = buffers[sweep % 2], buffers[1 - sweep % 2]

        def slices(step, carry, source=source, target=target, begin=HALF + 1 + sweep):
            for x in range(2):
                advance(begin + 2 * step + x, source, coef, surface_ref, keep_in(target))
            return carry

        lax.fori_loop(0, ROWS // 2 - 1 - sweep, slices, 0)


def outer_kernel(
    pairs_all,
    omega_ref,
    place_ref,
    below_ref,
    above_ref,
    one_in,
    two_in,
    coef_in,
    surface_ref,
    forward_ref,
    out_ref,
    term_ref,
    one,
    two,
    coef,
):
    omega = omega_ref[0]
    scale = omega * (1.0 / math.sqrt(pairs_all))

    for base, ref, inside in quarters(place_ref, below_ref, above_ref):

        def fill(x, carry, base=base, ref=ref, inside=inside):
            for side in range(2):
                for part in range(2):
                    for field in range(FIELDS):
                        value = jnp.where(inside, packed(ref, x, field, side, part), 0.0)
                        one[field, base + x, side, 8 + 8 * part : 16 + 8 * part] = value
                    value = packed(ref, x, FIELDS, side, part)
                    set_weights(coef, omega, value, base + x, side, part, inside)
            return carry

        lax.fori_loop(0, HALF, fill, 0)

    def give_out(x, side, part, news):
        base = side * 8 + x - HALF
        total = None
        for comp, (new_re, new_im) in enumerate(news):
            re_at = pl.ds((comp * LEVELS + 8 * part) * WIDE + base, 8, stride=WIDE)
            im_at = pl.ds(((3 + comp) * LEVELS + 8 * part) * WIDE + base, 8, stride=WIDE)
            out_ref[re_at, :] = new_re
            out_ref[im_at, :] = new_im
            piece = forward_ref[re_at, :] * new_im + forward_ref[im_at, :] * new_re
            total = piece if total is None else total + piece
        term_ref[pl.ds(8 * part * WIDE + base, 8, stride=WIDE), :] = total * scale

    buffers = (one, two)
    for sweep in range(SWEEPS):
        source, target = buffers[sweep % 2], buffers[1 - sweep % 2]
        emit = give_out if sweep == SWEEPS - 1 else keep_in(target)

        def slices(step, carry, source=source, emit=emit, sweep=sweep):
            for x in range(2):
                advance(1 + sweep + 2 * step + x, source, coef, surface_ref, emit)
                advance(WIDE - 1 - HALF - sweep + 2 * step + x, source, coef, surface_ref, emit)
            return carry

        lax.fori_loop(0, HALF // 2, slices, 0)


def body(
    omega, conductivity, forward_field, adjoint_start, station_data, station_owner, station_cell
):
    listed = station_cell.shape[0]
    tiles = lax.axis_size("tile")
    groups = lax.axis_size("freq")
    place = jnp.stack([lax.axis_index("tile"), jnp.int32(tiles)])

    vmem = pl.BlockSpec(memory_space=pltpu.VMEM)
    smem = pl.BlockSpec(memory_space=pltpu.SMEM)

    far = pl.BlockSpec(memory_space=pltpu.HBM)
    sent = pl.pallas_call(
        lists_kernel,
        out_shape=jax.ShapeDtypeStruct((tiles, 6 * listed // 128, 128), f32),
        in_specs=[far] * 3,
        out_specs=far,
        scratch_shapes=[
            pltpu.VMEM((2, 2, listed), f32),
            pltpu.VMEM((1, listed), jnp.int32),
            pltpu.VMEM((1, listed), jnp.int32),
            pltpu.VMEM((6 * listed // 128, 128), f32),
            pltpu.SemaphoreType.DMA((3,)),
            pltpu.SemaphoreType.DMA((tiles,)),
        ],
        cost_estimate=pl.CostEstimate(flops=10**9, bytes_accessed=10**6, transcendentals=0),
        name="lists",
    )(station_data.reshape(2, 2, listed), station_owner.reshape(1, listed), station_cell.reshape(1, listed))
    first, last = pl.pallas_call(
        pack_kernel,
        out_shape=(jax.ShapeDtypeStruct((HALO, 128), f32), jax.ShapeDtypeStruct((HALO, 128), f32)),
        in_specs=[vmem] * 2,
        out_specs=(vmem, vmem),
        compiler_params=pltpu.CompilerParams(vmem_limit_bytes=1 << 20),
        name="pack",
    )(as_lines(adjoint_start), as_lines(conductivity))
    below = lax.ppermute(last, "tile", [(i, (i + 1) % tiles) for i in range(tiles)])
    above = lax.ppermute(first, "tile", [((i + 1) % tiles, i) for i in range(tiles)])
    got = lax.all_to_all(sent, "tile", 0, 0, tiled=True)

    state_shape = jax.ShapeDtypeStruct((FIELDS, WIDE, 2, 32, 128), f32)
    coef_shape = jax.ShapeDtypeStruct((2, WIDE, 2, LEVELS, 128), f32)
    surface = pl.pallas_call(
        surface_kernel,
        out_shape=jax.ShapeDtypeStruct((4, WIDE, 2, 8, 128), f32),
        in_specs=[smem, vmem],
        out_specs=vmem,
        scratch_shapes=[pltpu.VMEM((128, ALONG), f32)],
        compiler_params=pltpu.CompilerParams(vmem_limit_bytes=4 << 20),
        cost_estimate=pl.CostEstimate(flops=10**9, bytes_accessed=10**6, transcendentals=0),
        name="surface",
    )(place, got)
    one, two, coef = pl.pallas_call(
        inner_kernel,
        out_shape=(state_shape, state_shape, coef_shape),
        in_specs=[smem, vmem, vmem, vmem],
        out_specs=(vmem,) * 3,
        compiler_params=pltpu.CompilerParams(vmem_limit_bytes=4 << 20),
        cost_estimate=pl.CostEstimate(flops=10**9, bytes_accessed=10**6, transcendentals=0),
        name="inner",
    )(omega, as_lines(adjoint_start), as_lines(conductivity), surface)

    adjoint, term, *_ = pl.pallas_call(
        functools.partial(outer_kernel, groups),
        out_shape=(
            jax.ShapeDtypeStruct((LINES, 128), f32),
            jax.ShapeDtypeStruct((LEVELS * WIDE, 128), f32),
            state_shape,
            state_shape,
            coef_shape,
        ),
        in_specs=[smem, smem] + [vmem] * 7,
        out_specs=(vmem,) * 5,
        input_output_aliases={4: 2, 5: 3, 6: 4},
        compiler_params=pltpu.CompilerParams(vmem_limit_bytes=4 << 20),
        name="outer",
    )(omega, place, below, above, one, two, coef, surface, as_lines(forward_field))

    terms = lax.all_to_all(term.reshape(groups, -1, 128), "freq", 0, 0, tiled=True)
    gradient = from_lines(terms.sum(axis=0))
    adjoint = pl.pallas_call(
        store_kernel,
        out_shape=jax.ShapeDtypeStruct((LINES, 128), f32),
        in_specs=[vmem],
        out_specs=far,
        scratch_shapes=[pltpu.SemaphoreType.DMA((8,))],
        compiler_params=pltpu.CompilerParams(vmem_limit_bytes=1 << 20),
        name="store",
    )(adjoint)
    return (from_lines(adjoint).reshape(adjoint_start.shape), gradient)


def solution(mesh):
    return jax.shard_map(
        body,
        mesh=mesh,
        in_specs=(
            P("freq"),
            P(None, "tile", None),
            P("freq", None, None, None, "tile", None),
            P("freq", None, None, None, "tile", None),
            P("freq", None, None, "tile"),
            P("tile", None),
            P("tile"),
        ),
        out_specs=(P("freq", None, None, None, "tile", None), P("freq", "tile", None)),
        check_vma=False,
    )
```

time: 55.3 us -> 52.4 us (0.948)
  blocking collectives: 15 us -> 0 us
  starting transfers between devices: 13.8 us -> 21.7 us
  waiting for transfers between devices: 7.91 us -> 13.3 us
  Pallas kernels: 16.2 us -> 15 us
    all_to_all x1 -> x0, blocking collectives: 15 us -> none  [body(): lax.all_to_all(term.reshape(groups, -1, 128), 'freq', 0, 0, tiled=True)]
    all_to_all x0 -> x1, starting transfers between devices: none -> 7.96 us  [body(): lax.all_to_all(term.reshape(groups, -1, 128), 'freq', 0, 0, tiled=True)]
    all_to_all x0 -> x1, waiting for transfers between devices: none -> 6.73 us  [body(): lax.all_to_all(term.reshape(groups, -1, 128), 'freq', 0, 0, tiled=True)]
    ppermute x1, waiting for transfers between devices: 6.89 us -> 4.28 us  [body(): lax.ppermute(last, 'tile', [(i, (i + 1) % tiles) for i in range(tiles)])]
    all_to_all x1, waiting for transfers between devices: 1.02 us -> 2.24 us  [body(): got = lax.all_to_all(sent, 'tile', 0, 0, tiled=True)]
    pallas_call x1, Pallas kernels: 2.11 us -> 1.04 us  [body(): pl.pallas_call(pack_kernel, out_shape=(jax.ShapeDtypeStruct((HALO, 128),...]
    pallas_call x2 -> x3, Pallas kernels: 8.25 us -> 8.05 us  [the longest x1 5.16 us: body(): pl.pallas_call(functools.partial(outer_kernel, groups), out_shape=(jax.Sh...]
  transfers between devices with their start and end apart: 3 -> 4, of which waited for: 2 -> 3; matrix products, arithmetic and copies ran while one was open for 0% -> 0% of each run, Pallas kernels for 12% -> 16%
where the time goes in v3:
time: 52.4 us; the launch traced here: 52 us
  starting transfers between devices  21.7 us (41%)
  Pallas kernels  15 us (29%)
  waiting for transfers between devices  13.3 us (25%)
  between operations  1.36 us (3%)
  other arithmetic  0.69 us (1%)
    all_to_all x1, starting transfers between devices, body(): got = lax.all_to_all(sent, 'tile', 0, 0, tiled=True)  10.1 us
    all_to_all x1, starting transfers between devices, body(): lax.all_to_all(term.reshape(groups, -1, 128), 'freq', 0, 0, tiled=True)  7.96 us
    all_to_all x1, waiting for transfers between devices, body(): lax.all_to_all(term.reshape(groups, -1, 128), 'freq', 0, 0, tiled=True)  6.73 us
    pallas_call x1, Pallas kernels, body(): pl.pallas_call(functools.partial(outer_kernel, groups), out_shape=(jax.Sh...  5.16 us
    pallas_call x1, Pallas kernels, body(): pl.pallas_call(surface_kernel, out_shape=jax.ShapeDtypeStruct((4, WIDE, 2...  4.3 us
    ppermute x1, waiting for transfers between devices, body(): lax.ppermute(last, 'tile', [(i, (i + 1) % tiles) for i in range(tiles)])  4.28 us
    all_to_all x1, waiting for transfers between devices, body(): got = lax.all_to_all(sent, 'tile', 0, 0, tiled=True)  2.24 us
    ppermute x1, starting transfers between devices, body(): lax.ppermute(first, 'tile', [((i + 1) % tiles, i) for i in range(tiles)])  2.21 us
  transfers between devices with their start and end apart: 4, of which 3 were waited for; matrix products, arithmetic and copies ran while one was open for 0% of the time, Pallas kernels for 16%

profile of v3, /device:TPU:1, one launch (start us, length us, event | category | flops | bytes accessed | tf_op | source)
XLA Modules:
  0.0 52.0 jit_solution(4520294906999758032)
XLA Ops:
  0.6 0.0 copy-start.1
  0.6 0.0 copy-start.2
  0.7 1.6 %lists.1 = f32[16,24,128]{2,1,0:T(8,128)} custom-call(f32[2,2,512]{2,1,0:T(2,128)} %bitcast.37, s32[1,512]{1,0:T(1,128)} %bitcast.38, s32[1,512]{1,0:T(1,128)} %bitcast.39), custom_call_target="tpu_custom_call" | custom-call | flops 1000000000 | bytes 1000000 | tf_op jit(solution)/shard_map/lists/pallas_call | solution.py:330
  2.3 10.1 %all-to-all-start = ((f32[16,24,128]{2,1,0:T(8,128)}), f32[16,24,128]{2,1,0:T(8,128)S(1)}, u32[]{:S(2)}, u32[]{:S(2)}) async-start(f32[16,24,128]{2,1,0:T(8,128)} %lists.1), calls=%async_computation | async-start | bytes 393216 | tf_op jit(solution)/shard_map/all_to_all | solution.py:356
  12.5 0.0 copy-done.1
  12.5 0.0 copy-done.2
  12.5 1.0 %pack.1 = (f32[896,128]{1,0:T(8,128)S(1)}, f32[896,128]{1,0:T(8,128)}) custom-call(f32[1536,128]{1,0:T(8,128)S(1)} %bitcast.31, f32[256,128]{1,0:T(8,128)S(1)} %bitcast.33), custom_call_target="tpu_custom_call" | custom-call | tf_op jit(solution)/shard_map/pack/pallas_call | solution.py:346
  13.5 1.4 %collective-permute-start = (f32[896,128]{1,0:T(8,128)}, f32[896,128]{1,0:T(8,128)S(1)}, u32[]{:S(2)}, u32[]{:S(2)}) collective-permute-start(f32[896,128]{1,0:T(8,128)} %get-tuple-element.9), channel_id=1, source_target_pairs={{0,1},{1,2},{2,3},{3,4},{4,5},{5,6},{6,7},{7,8},{8,9},{9,10},{10,1... | collective-permute-start | bytes 1376264 | tf_op jit(solution)/shard_map/ppermute | solution.py:354
  14.9 2.2 %collective-permute-start.1 = (f32[896,128]{1,0:T(8,128)S(1)}, f32[896,128]{1,0:T(8,128)S(1)}, u32[]{:S(2)}, u32[]{:S(2)}) collective-permute-start(f32[896,128]{1,0:T(8,128)S(1)} %get-tuple-element.10), channel_id=1, source_target_pairs={{1,0},{2,1},{3,2},{4,3},{5,4},{6,5},{7,6},{8,7},{9,8},{10,9},{11,1... | collective-permute-start | bytes 1376264 | tf_op jit(solution)/shard_map/ppermute | solution.py:355
  17.8 0.1 pad_add_fusion.place_ref
  17.8 0.0 copy-start
  17.8 2.2 %all-to-all-done.lists_ref = f32[16,24,128]{2,1,0:T(8,128)S(1)} async-done(((f32[16,24,128]{2,1,0:T(8,128)}), f32[16,24,128]{2,1,0:T(8,128)S(1)}, u32[]{:S(2)}, u32[]{:S(2)}) %all-to-all-start) | async-done | bytes 196640 | tf_op jit(solution)/shard_map/all_to_all | solution.py:356
  20.1 4.3 %surface.1.surface_ref = f32[4,16,2,8,128]{4,3,2,1,0:T(8,128)S(1)} custom-call(s32[2]{0:T(128)S(1)} %pad_add_fusion.place_ref, f32[16,24,128]{2,1,0:T(8,128)S(1)} %all-to-all-done.lists_ref), custom_call_target="tpu_custom_call" | custom-call | flops 1000000000 | bytes 1000000 | tf_op jit(solution)/shard_map/surface/pallas_call | solution.py:360
  24.4 2.0 %inner.1 = (f32[6,16,2,32,128]{4,3,2,1,0:T(8,128)S(1)}, f32[6,16,2,32,128]{4,3,2,1,0:T(8,128)S(1)}, f32[2,16,2,16,128]{4,3,2,1,0:T(8,128)S(1)}) custom-call(f32[1]{0:T(128)S(6)} %copy.15.omega_ref, f32[1536,128]{1,0:T(8,128)S(1)} %bitcast.32, f32[256,128]{1,0:T(8,128)S(1)} %bitcast.34, f32[4,16,2,8,128]{4,3,2,1,0:T(8,128)S(1)} %surface.1.surface_ref), custom_call_target="tpu_custom_call" | custom-call | flops 1000000000 | bytes 1000000 | tf_op jit(solution)/shard_map/inner/pallas_call | solution.py:370
  26.3 4.3 %collective-permute-done.below_ref = f32[896,128]{1,0:T(8,128)S(1)} collective-permute-done((f32[896,128]{1,0:T(8,128)}, f32[896,128]{1,0:T(8,128)S(1)}, u32[]{:S(2)}, u32[]{:S(2)}) %collective-permute-start) | collective-permute-done | bytes 458784 | tf_op jit(solution)/shard_map/ppermute | solution.py:354
  30.6 0.0 collective-permute-done.1.above_ref
  30.6 0.0 copy-done
  30.6 5.2 %outer.1 = (f32[1536,128]{1,0:T(8,128)S(1)}, f32[256,128]{1,0:T(8,128)}, f32[6,16,2,32,128]{4,3,2,1,0:T(8,128)S(1)}, f32[6,16,2,32,128]{4,3,2,1,0:T(8,128)S(1)}, f32[2,16,2,16,128]{4,3,2,1,0:T(8,128)S(1)}) custom-call(f32[1]{0:T(128)S(6)} %copy.15.omega_ref, s32[2]{0:T(128)S(1)} %pad_add_fusion.place_ref, ...), custom_call_target="tpu_custom_call", output_to_operand_aliasing={{2}: (4, {}), {3}: (5, {}), {4}: (6, {})} | custom-call | tf_op jit(solution)/shard_map/outer/pallas_call | solution.py:380
  35.8 8.0 %all-to-all-start.1 = ((f32[16,16,128]{2,1,0:T(8,128)}), f32[16,16,128]{2,1,0:T(8,128)S(1)}, u32[]{:S(2)}, u32[]{:S(2)}) async-start(f32[16,16,128]{2,1,0:T(8,128)} %bitcast.20), calls=%async_computation.1 | async-start | bytes 262144 | tf_op jit(solution)/shard_map/all_to_all | solution.py:396
  43.7 0.9 %store.1 = f32[1536,128]{1,0:T(8,128)} custom-call(f32[1536,128]{1,0:T(8,128)S(1)} %get-tuple-element.14.value_ref), custom_call_target="tpu_custom_call" | custom-call | tf_op jit(solution)/shard_map/store/pallas_call | solution.py:398
  44.7 6.7 %all-to-all-done.1 = f32[16,16,128]{2,1,0:T(8,128)S(1)} async-done(((f32[16,16,128]{2,1,0:T(8,128)}), f32[16,16,128]{2,1,0:T(8,128)S(1)}, u32[]{:S(2)}, u32[]{:S(2)}) %all-to-all-start.1) | async-done | bytes 131104 | tf_op jit(solution)/shard_map/all_to_all | solution.py:396
  51.4 0.6 %reduce_sum.9 = f32[16,128]{1,0:T(8,128)} reduce(f32[16,16,128]{2,1,0:T(8,128)S(1)} %all-to-all-done.1, f32[]{:T(128)} %constant.2.clone.1), dimensions={0}, to_apply=%region_0.0 | reduce | flops 30720 | bytes 139268 | tf_op jit(solution)/shard_map/reduce_sum | solution.py:397
Async XLA Ops:
  0.6 11.8 %copy-start.1 = (f32[1,2,3,16,8,256]{5,4,3,2,1,0:T(8,128)S(1)}, f32[1,2,3,16,8,256]{5,4,3,2,1,0:T(8,128)}, u32[]{:S(2)}) copy-start(f32[1,2,3,16,8,256]{5,4,3,2,1,0:T(8,128)} %param.10) | copy-start | bytes 2359300
  0.6 11.8 %copy-start.2 = (f32[16,8,256]{2,1,0:T(8,128)S(1)}, f32[16,8,256]{2,1,0:T(8,128)}, u32[]{:S(2)}) copy-start(f32[16,8,256]{2,1,0:T(8,128)} %param.8) | copy-start | bytes 393220
  2.3 17.8 %all-to-all-start = ((f32[16,24,128]{2,1,0:T(8,128)}), f32[16,24,128]{2,1,0:T(8,128)S(1)}, u32[]{:S(2)}, u32[]{:S(2)}) async-start(f32[16,24,128]{2,1,0:T(8,128)} %lists.1), calls=%async_computation | async-start | bytes 393216 | tf_op jit(solution)/shard_map/all_to_all | solution.py:356
  13.5 17.1 %collective-permute-start = (f32[896,128]{1,0:T(8,128)}, f32[896,128]{1,0:T(8,128)S(1)}, u32[]{:S(2)}, u32[]{:S(2)}) collective-permute-start(f32[896,128]{1,0:T(8,128)} %get-tuple-element.9), channel_id=1, source_target_pairs={{0,1},{1,2},{2,3},{3,4},{4,5},{5,6},{6,7},{7,8},{8,9},{9,10},{10,1... | collective-permute-start | bytes 1376264 | tf_op jit(solution)/shard_map/ppermute | solution.py:354
  14.9 15.7 %collective-permute-start.1 = (f32[896,128]{1,0:T(8,128)S(1)}, f32[896,128]{1,0:T(8,128)S(1)}, u32[]{:S(2)}, u32[]{:S(2)}) collective-permute-start(f32[896,128]{1,0:T(8,128)S(1)} %get-tuple-element.10), channel_id=1, source_target_pairs={{1,0},{2,1},{3,2},{4,3},{5,4},{6,5},{7,6},{8,7},{9,8},{10,9},{11,1... | collective-permute-start | bytes 1376264 | tf_op jit(solution)/shard_map/ppermute | solution.py:355
  17.8 12.8 %copy-start = (f32[1,2,3,16,8,256]{5,4,3,2,1,0:T(8,128)S(1)}, f32[1,2,3,16,8,256]{5,4,3,2,1,0:T(8,128)}, u32[]{:S(2)}) copy-start(f32[1,2,3,16,8,256]{5,4,3,2,1,0:T(8,128)} %param.9) | copy-start | bytes 2359300
  35.8 15.6 %all-to-all-start.1 = ((f32[16,16,128]{2,1,0:T(8,128)}), f32[16,16,128]{2,1,0:T(8,128)S(1)}, u32[]{:S(2)}, u32[]{:S(2)}) async-start(f32[16,16,128]{2,1,0:T(8,128)} %bitcast.20), calls=%async_computation.1 | async-start | bytes 262144 | tf_op jit(solution)/shard_map/all_to_all | solution.py:396

commit v4 on v3

--- a/solution.py
+++ b/solution.py
@@ -31,8 +31,22 @@
     return lines.reshape(-1, 2, ROWS, 128).transpose(0, 2, 1, 3).reshape(-1, ROWS, ALONG)
 
 
-def pack_kernel(field_ref, sigma_ref, first_ref, last_ref):
+def pack_kernel(field_hbm, sigma_hbm, first_hbm, last_hbm, field_ref, sigma_ref, first_ref, last_ref, in_sems, out_sems):
+    size = LEVELS * WIDE
+    block = HALF * 2 * LEVELS
+    pairs = [
+        (field_hbm.at[pl.ds(kind * size, size)], field_ref.at[pl.ds(kind * size, size)])
+        for kind in range(FIELDS)
+    ]
+    pairs.append((sigma_hbm, sigma_ref))
+    copies = [
+        pltpu.make_async_copy(source, target, in_sems.at[which]) for which, (source, target) in enumerate(pairs)
+    ]
+    for copy in copies:
+        copy.start()
+    sends = []
     for kind in range(KINDS):
+        copies[kind].wait()
         source, base = (field_ref, kind * LEVELS) if kind < FIELDS else (sigma_ref, 0)
         for x in range(ROWS):
             target = first_ref if x < HALF else last_ref
@@ -41,6 +55,13 @@
                     start = (base + 8 * part) * WIDE + side * 8 + x
                     place = ((kind * HALF + x % HALF) * 2 + side) * LEVELS + 8 * part
                     target[place : place + 8] = source[pl.ds(start, 8, stride=WIDE), :]
+        rows = pl.ds(kind * block, block)
+        for which, (source, target) in enumerate(((first_ref, first_hbm), (last_ref, last_hbm))):
+            copy = pltpu.make_async_copy(source.at[rows], target.at[rows], out_sems.at[2 * kind + which])
+            copy.start()
+            sends.append(copy)
+    for copy in sends:
+        copy.wait()
 
 
 def lists_kernel(data_hbm, owner_hbm, cell_hbm, sent_hbm, data_ref, owner_ref, cell_ref, block_ref, in_sems, out_sems):
@@ -115,8 +136,8 @@
     ]
 
 
-def advance(x, source, coef, surface_ref, emit):
-    for part in range(2):
+def advance(x, source, coef, emit, surface_ref=None, parts=(0, 1)):
+    for part in parts:
         row = 8 + 8 * part
         off, old = [], []
         for half in range(2):
@@ -151,7 +172,7 @@
             for comp in range(3):
                 sums = y_sum(ahead[comp], behind[comp])
                 value = [rest[comp][side] + sums[side] for side in range(2)]
-                if part == 0 and comp < 2:
+                if part == 0 and comp < 2 and surface_ref is not None:
                     value = [value[side] + surface_ref[2 * half + comp, x, side] for side in range(2)]
                 off.append(value)
         for side in range(2):
@@ -175,7 +196,11 @@
     return emit
 
 
-def surface_kernel(place_ref, lists_ref, out_ref, acc_ref):
+def source_kernel(
+    pairs_all, omega_ref, place_ref, lists_ref, coef, forward_ref, out_in, term_in,
+    out_ref, term_ref, acc_ref, surface_ref, three, four,
+):
+    scale = omega_ref[0] * (1.0 / math.sqrt(pairs_all))
     start = place_ref[0] * ROWS - HALF
     sources = lists_ref.shape[0]
     chunks = lists_ref.shape[1] // 6
@@ -206,17 +231,65 @@
         )
         return carry
 
-    lax.fori_loop(0, sources, step, 0)
+    lax.fori_loop(0, sources, step, 0, unroll=8)
     top = lax.broadcasted_iota(jnp.int32, (8, 128), 0) == 0
     for which in range(4):
         total = acc_ref[32 * which : 32 * which + 16] + acc_ref[32 * which + 16 : 32 * which + 32]
         for x in range(WIDE):
             for side in range(2):
                 line = total[x : x + 1, 128 * side : 128 * side + 128]
-                out_ref[which, x, side] = jnp.where(top, line, 0.0)
-
-
-def inner_kernel(omega_ref, field_ref, sigma_ref, surface_ref, one, two, coef):
+                surface_ref[which, x, side] = jnp.where(top, line, 0.0)
+
+    zero = jnp.zeros((8, 128), f32)
+
+    def clear(x, carry):
+        for side in range(2):
+            for field in range(FIELDS):
+                for buffer in (three, four):
+                    buffer[field, x, side, 0:8] = zero
+                    buffer[field, x, side, 16:24] = zero
+            three[2, x, side, 8:16] = zero
+            three[5, x, side, 8:16] = zero
+        return carry
+
+    lax.fori_loop(1, WIDE - 1, clear, 0, unroll=2)
+    for x in range(1, WIDE - 1):
+        for side in range(2):
+            c1, c2 = coef[0, x, side, 0:8], coef[1, x, side, 0:8]
+            for comp in range(2):
+                re, im = surface_ref[comp, x, side], surface_ref[2 + comp, x, side]
+                three[comp, x, side, 8:16] = c1 * re - c2 * im
+                three[3 + comp, x, side, 8:16] = c2 * re + c1 * im
+
+    def add_out(x, side, part, news):
+        base = side * 8 + x - HALF
+        total = None
+        for comp, (new_re, new_im) in enumerate(news):
+            re_at = pl.ds(comp * LEVELS * WIDE + base, 8, stride=WIDE)
+            im_at = pl.ds((3 + comp) * LEVELS * WIDE + base, 8, stride=WIDE)
+            out_ref[re_at, :] = out_ref[re_at, :] + new_re
+            out_ref[im_at, :] = out_ref[im_at, :] + new_im
+            piece = forward_ref[re_at, :] * new_im + forward_ref[im_at, :] * new_re
+            total = piece if total is None else total + piece
+        at = pl.ds(base, 8, stride=WIDE)
+        term_ref[at, :] = term_in[at, :] + total * scale
+
+    half = LEVELS * WIDE // 2
+    term_ref[half : 2 * half] = term_in[half : 2 * half]
+    buffers = (four, three)
+    for sweep in range(1, SWEEPS):
+        source, target = buffers[sweep % 2], buffers[1 - sweep % 2]
+        emit = add_out if sweep == SWEEPS - 1 else keep_in(target)
+
+        def slices(step, carry, source=source, emit=emit, begin=1 + sweep):
+            for x in range(2):
+                advance(begin + 2 * step + x, source, coef, emit, surface_ref, (0,))
+            return carry
+
+        lax.fori_loop(0, (WIDE - 2 - 2 * sweep) // 2, slices, 0, unroll=(3, 5, 4)[sweep - 1])
+
+
+def inner_kernel(omega_ref, field_ref, sigma_ref, one, two, coef):
     omega = omega_ref[0]
     zero = jnp.zeros((8, 128), f32)
 
@@ -249,10 +322,10 @@
 
         def slices(step, carry, source=source, target=target, begin=HALF + 1 + sweep):
             for x in range(2):
-                advance(begin + 2 * step + x, source, coef, surface_ref, keep_in(target))
+                advance(begin + 2 * step + x, source, coef, keep_in(target))
             return carry
 
-        lax.fori_loop(0, ROWS // 2 - 1 - sweep, slices, 0)
+        lax.fori_loop(0, ROWS // 2 - 1 - sweep, slices, 0, unroll=ROWS // 2 - 1 - sweep)
 
 
 def outer_kernel(
@@ -264,7 +337,6 @@
     one_in,
     two_in,
     coef_in,
-    surface_ref,
     forward_ref,
     out_ref,
     term_ref,
@@ -308,11 +380,11 @@
 
         def slices(step, carry, source=source, emit=emit, sweep=sweep):
             for x in range(2):
-                advance(1 + sweep + 2 * step + x, source, coef, surface_ref, emit)
-                advance(WIDE - 1 - HALF - sweep + 2 * step + x, source, coef, surface_ref, emit)
+                advance(1 + sweep + 2 * step + x, source, coef, emit)
+                advance(WIDE - 1 - HALF - sweep + 2 * step + x, source, coef, emit)
             return carry
 
-        lax.fori_loop(0, HALF // 2, slices, 0)
+        lax.fori_loop(0, HALF // 2, slices, 0, unroll=2)
 
 
 def body(
@@ -345,10 +417,20 @@
     )(station_data.reshape(2, 2, listed), station_owner.reshape(1, listed), station_cell.reshape(1, listed))
     first, last = pl.pallas_call(
         pack_kernel,
-        out_shape=(jax.ShapeDtypeStruct((HALO, 128), f32), jax.ShapeDtypeStruct((HALO, 128), f32)),
-        in_specs=[vmem] * 2,
-        out_specs=(vmem, vmem),
-        compiler_params=pltpu.CompilerParams(vmem_limit_bytes=1 << 20),
+        out_shape=(
+            jax.ShapeDtypeStruct((HALO, 128), f32),
+            jax.ShapeDtypeStruct((HALO, 128), f32),
+        ),
+        in_specs=[far] * 2,
+        out_specs=(far, far),
+        scratch_shapes=[
+            pltpu.VMEM((LINES, 128), f32),
+            pltpu.VMEM((LEVELS * WIDE, 128), f32),
+            pltpu.VMEM((HALO, 128), f32),
+            pltpu.VMEM((HALO, 128), f32),
+            pltpu.SemaphoreType.DMA((KINDS,)),
+            pltpu.SemaphoreType.DMA((2 * KINDS,)),
+        ],
         name="pack",
     )(as_lines(adjoint_start), as_lines(conductivity))
     below = lax.ppermute(last, "tile", [(i, (i + 1) % tiles) for i in range(tiles)])
@@ -357,41 +439,47 @@
 
     state_shape = jax.ShapeDtypeStruct((FIELDS, WIDE, 2, 32, 128), f32)
     coef_shape = jax.ShapeDtypeStruct((2, WIDE, 2, LEVELS, 128), f32)
-    surface = pl.pallas_call(
-        surface_kernel,
-        out_shape=jax.ShapeDtypeStruct((4, WIDE, 2, 8, 128), f32),
-        in_specs=[smem, vmem],
-        out_specs=vmem,
-        scratch_shapes=[pltpu.VMEM((128, ALONG), f32)],
-        compiler_params=pltpu.CompilerParams(vmem_limit_bytes=4 << 20),
-        cost_estimate=pl.CostEstimate(flops=10**9, bytes_accessed=10**6, transcendentals=0),
-        name="surface",
-    )(place, got)
+    cost = pl.CostEstimate(flops=10**9, bytes_accessed=10**6, transcendentals=0)
     one, two, coef = pl.pallas_call(
         inner_kernel,
         out_shape=(state_shape, state_shape, coef_shape),
-        in_specs=[smem, vmem, vmem, vmem],
+        in_specs=[smem, vmem, vmem],
         out_specs=(vmem,) * 3,
         compiler_params=pltpu.CompilerParams(vmem_limit_bytes=4 << 20),
-        cost_estimate=pl.CostEstimate(flops=10**9, bytes_accessed=10**6, transcendentals=0),
+        cost_estimate=cost,
         name="inner",
-    )(omega, as_lines(adjoint_start), as_lines(conductivity), surface)
-
-    adjoint, term, *_ = pl.pallas_call(
+    )(omega, as_lines(adjoint_start), as_lines(conductivity))
+
+    lines_shape = jax.ShapeDtypeStruct((LINES, 128), f32)
+    term_shape = jax.ShapeDtypeStruct((LEVELS * WIDE, 128), f32)
+    forward = as_lines(forward_field)
+    adjoint, term, _, _, coef = pl.pallas_call(
         functools.partial(outer_kernel, groups),
-        out_shape=(
-            jax.ShapeDtypeStruct((LINES, 128), f32),
-            jax.ShapeDtypeStruct((LEVELS * WIDE, 128), f32),
-            state_shape,
-            state_shape,
-            coef_shape,
-        ),
-        in_specs=[smem, smem] + [vmem] * 7,
+        out_shape=(lines_shape, term_shape, state_shape, state_shape, coef_shape),
+        in_specs=[smem, smem] + [vmem] * 6,
         out_specs=(vmem,) * 5,
         input_output_aliases={4: 2, 5: 3, 6: 4},
         compiler_params=pltpu.CompilerParams(vmem_limit_bytes=4 << 20),
+        cost_estimate=cost,
         name="outer",
-    )(omega, place, below, above, one, two, coef, surface, as_lines(forward_field))
+    )(omega, place, below, above, one, two, coef, forward)
+
+    adjoint, term = pl.pallas_call(
+        functools.partial(source_kernel, groups),
+        out_shape=(lines_shape, term_shape),
+        in_specs=[smem, smem] + [vmem] * 5,
+        out_specs=(vmem,) * 2,
+        scratch_shapes=[
+            pltpu.VMEM((128, ALONG), f32),
+            pltpu.VMEM((4, WIDE, 2, 8, 128), f32),
+            pltpu.VMEM((FIELDS, WIDE, 2, 24, 128), f32),
+            pltpu.VMEM((FIELDS, WIDE, 2, 24, 128), f32),
+        ],
+        input_output_aliases={5: 0},
+        compiler_params=pltpu.CompilerParams(vmem_limit_bytes=10 << 20),
+        cost_estimate=cost,
+        name="source",
+    )(omega, place, got, coef, forward, adjoint, term)
 
     terms = lax.all_to_all(term.reshape(groups, -1, 128), "freq", 0, 0, tiled=True)
     gradient = from_lines(terms.sum(axis=0))

time: 52.4 us -> 49.5 us (0.945)
  waiting for transfers between devices: 13.3 us -> 7.43 us
  starting transfers between devices: 21.7 us -> 23.7 us
  Pallas kernels: 15 us -> 16 us
    all_to_all x1, starting transfers between devices: 10.1 us -> 5.31 us  [body(): got = lax.all_to_all(sent, 'tile', 0, 0, tiled=True)]
    ppermute x1, waiting for transfers between devices: 4.28 us -> 0.69 us  [body(): lax.ppermute(last, 'tile', [(i, (i + 1) % tiles) for i in range(tiles)])]
    all_to_all x1, starting transfers between devices: 7.96 us -> 10.8 us  [body(): lax.all_to_all(term.reshape(groups, -1, 128), 'freq', 0, 0, tiled=True)]
    ppermute x1, starting transfers between devices: 2.21 us -> 5.04 us  [body(): lax.ppermute(first, 'tile', [((i + 1) % tiles, i) for i in range(tiles)])]
    all_to_all x1, waiting for transfers between devices: 2.24 us -> 0.01 us  [body(): got = lax.all_to_all(sent, 'tile', 0, 0, tiled=True)]
    ppermute x1, starting transfers between devices: 1.36 us -> 2.54 us  [body(): lax.ppermute(last, 'tile', [(i, (i + 1) % tiles) for i in range(tiles)])]
    pallas_call x1, Pallas kernels: 1.04 us -> 2.18 us  [body(): pl.pallas_call(pack_kernel, out_shape=(jax.ShapeDtypeStruct((HALO, 128),...]
  transfers between devices with their start and end apart: 4 -> 4, of which waited for: 3 -> 2; matrix products, arithmetic and copies ran while one was open for 0% -> 0% of each run, Pallas kernels for 16% -> 19%
where the time goes in v4:
time: 49.5 us; the launch traced here: 49.2 us
  starting transfers between devices  23.7 us (48%)
  Pallas kernels  16 us (32%)
  waiting for transfers between devices  7.43 us (15%)
  between operations  1.37 us (3%)
  other arithmetic  0.69 us (1%)
    all_to_all x1, starting transfers between devices, body(): lax.all_to_all(term.reshape(groups, -1, 128), 'freq', 0, 0, tiled=True)  10.8 us
    all_to_all x1, waiting for transfers between devices, body(): lax.all_to_all(term.reshape(groups, -1, 128), 'freq', 0, 0, tiled=True)  6.73 us
    all_to_all x1, starting transfers between devices, body(): got = lax.all_to_all(sent, 'tile', 0, 0, tiled=True)  5.31 us
    ppermute x1, starting transfers between devices, body(): lax.ppermute(first, 'tile', [((i + 1) % tiles, i) for i in range(tiles)])  5.04 us
    pallas_call x1, Pallas kernels, body(): pl.pallas_call(functools.partial(outer_kernel, groups), out_shape=(lines_...  4.69 us
    pallas_call x1, Pallas kernels, body(): pl.pallas_call(functools.partial(source_kernel, groups), out_shape=(lines...  4.62 us
    ppermute x1, starting transfers between devices, body(): lax.ppermute(last, 'tile', [(i, (i + 1) % tiles) for i in range(tiles)])  2.54 us
    pallas_call x1, Pallas kernels, body(): pl.pallas_call(pack_kernel, out_shape=(jax.ShapeDtypeStruct((HALO, 128),...  2.18 us
  transfers between devices with their start and end apart: 4, of which 2 were waited for; matrix products, arithmetic and copies ran while one was open for 0% of the time, Pallas kernels for 19%

profile of v4, /device:TPU:1, one launch (start us, length us, event | category | flops | bytes accessed | tf_op | source)
XLA Modules:
  0.0 49.2 jit_solution(10306123520527851178)
XLA Ops:
  0.6 0.0 copy-start.1
  0.6 0.0 copy-start.2
  0.6 2.2 %pack.1 = (f32[896,128]{1,0:T(8,128)}, f32[896,128]{1,0:T(8,128)}) custom-call(f32[1536,128]{1,0:T(8,128)} %bitcast.32, f32[256,128]{1,0:T(8,128)} %bitcast.34), custom_call_target="tpu_custom_call" | custom-call | tf_op jit(solution)/shard_map/pack/pallas_call | solution.py:418
  2.8 2.5 %collective-permute-start = (f32[896,128]{1,0:T(8,128)}, f32[896,128]{1,0:T(8,128)S(1)}, u32[]{:S(2)}, u32[]{:S(2)}) collective-permute-start(f32[896,128]{1,0:T(8,128)} %get-tuple-element.12), channel_id=1, source_target_pairs={{0,1},{1,2},{2,3},{3,4},{4,5},{5,6},{6,7},{7,8},{8,9},{9,10},{10,1... | collective-permute-start | bytes 1376264 | tf_op jit(solution)/shard_map/ppermute | solution.py:436
  5.4 5.0 %collective-permute-start.1 = (f32[896,128]{1,0:T(8,128)}, f32[896,128]{1,0:T(8,128)S(1)}, u32[]{:S(2)}, u32[]{:S(2)}) collective-permute-start(f32[896,128]{1,0:T(8,128)} %get-tuple-element.13), channel_id=1, source_target_pairs={{1,0},{2,1},{3,2},{4,3},{5,4},{6,5},{7,6},{8,7},{9,8},{10,9},{11,1... | collective-permute-start | bytes 1376264 | tf_op jit(solution)/shard_map/ppermute | solution.py:437
  10.4 0.0 copy-start
  10.4 1.6 %lists.1 = f32[16,24,128]{2,1,0:T(8,128)} custom-call(f32[2,2,512]{2,1,0:T(2,128)} %bitcast.38, s32[1,512]{1,0:T(1,128)} %bitcast.39, s32[1,512]{1,0:T(1,128)} %bitcast.40), custom_call_target="tpu_custom_call" | custom-call | flops 1000000000 | bytes 1000000 | tf_op jit(solution)/shard_map/lists/pallas_call | solution.py:402
  12.1 5.3 %all-to-all-start = ((f32[16,24,128]{2,1,0:T(8,128)}), f32[16,24,128]{2,1,0:T(8,128)S(1)}, u32[]{:S(2)}, u32[]{:S(2)}) async-start(f32[16,24,128]{2,1,0:T(8,128)} %lists.1), calls=%async_computation | async-start | bytes 393216 | tf_op jit(solution)/shard_map/all_to_all | solution.py:438
  18.0 0.0 copy-done.1
  18.0 0.0 copy-done.2
  18.1 2.0 %inner.1 = (f32[6,16,2,32,128]{4,3,2,1,0:T(8,128)S(1)}, f32[6,16,2,32,128]{4,3,2,1,0:T(8,128)S(1)}, f32[2,16,2,16,128]{4,3,2,1,0:T(8,128)S(1)}) custom-call(f32[1]{0:T(128)S(6)} %copy.17.omega_ref, f32[1536,128]{1,0:T(8,128)S(1)} %bitcast.33, f32[256,128]{1,0:T(8,128)S(1)} %bitcast.35), custom_call_target="tpu_custom_call" | custom-call | flops 1000000000 | bytes 1000000 | tf_op jit(solution)/shard_map/inner/pallas_call | solution.py:443
  20.0 0.1 pad_add_fusion.place_ref
  20.1 0.7 %collective-permute-done.below_ref = f32[896,128]{1,0:T(8,128)S(1)} collective-permute-done((f32[896,128]{1,0:T(8,128)}, f32[896,128]{1,0:T(8,128)S(1)}, u32[]{:S(2)}, u32[]{:S(2)}) %collective-permute-start) | collective-permute-done | bytes 458784 | tf_op jit(solution)/shard_map/ppermute | solution.py:436
  20.8 0.0 collective-permute-done.1.above_ref
  20.8 0.0 copy-done
  20.8 4.7 %outer.1 = (f32[1536,128]{1,0:T(8,128)S(1)}, f32[256,128]{1,0:T(8,128)S(1)}, f32[6,16,2,32,128]{4,3,2,1,0:T(8,128)S(1)}, f32[6,16,2,32,128]{4,3,2,1,0:T(8,128)S(1)}, f32[2,16,2,16,128]{4,3,2,1,0:T(8,128)S(1)}) custom-call(f32[1]{0:T(128)S(6)} %copy.17.omega_ref, ...), custom_call_target="tpu_custom_call", output_to_operand_aliasing={{2}: (4, {}), {3}: (5, {}), {4}: (6, {})} | custom-call | flops 1000000000 | bytes 1000000 | tf_op jit(solution)/shard_map/outer/pallas_call | solution.py:456
  25.5 0.0 all-to-all-done.lists_ref
  25.5 4.6 %source.1 = (f32[1536,128]{1,0:T(8,128)S(1)}, f32[256,128]{1,0:T(8,128)}) custom-call(f32[1]{0:T(128)S(6)} %copy.17.omega_ref, s32[2]{0:T(128)S(1)} %pad_add_fusion.place_ref, f32[16,24,128]{2,1,0:T(8,128)S(1)} %all-to-all-done.lists_ref, f32[2,16,2,16,128]{4,3,2,1,0:T(8,128)S(1)} %get-tuple-element.17.coef, ...), custom_call_target="tpu_custom_call", output_to_operand_aliasing={{0}: (5, {})} | custom-call | flops 1000000000 | bytes 1000000 | tf_op jit(solution)/shard_map/source/pallas_call | solution.py:467
  30.1 10.8 %all-to-all-start.1 = ((f32[16,16,128]{2,1,0:T(8,128)}), f32[16,16,128]{2,1,0:T(8,128)S(1)}, u32[]{:S(2)}, u32[]{:S(2)}) async-start(f32[16,16,128]{2,1,0:T(8,128)} %bitcast.20), calls=%async_computation.1 | async-start | bytes 262144 | tf_op jit(solution)/shard_map/all_to_all | solution.py:484
  40.9 0.9 %store.1 = f32[1536,128]{1,0:T(8,128)} custom-call(f32[1536,128]{1,0:T(8,128)S(1)} %get-tuple-element.20.value_ref), custom_call_target="tpu_custom_call" | custom-call | tf_op jit(solution)/shard_map/store/pallas_call | solution.py:486
  41.9 6.7 %all-to-all-done.1 = f32[16,16,128]{2,1,0:T(8,128)S(1)} async-done(((f32[16,16,128]{2,1,0:T(8,128)}), f32[16,16,128]{2,1,0:T(8,128)S(1)}, u32[]{:S(2)}, u32[]{:S(2)}) %all-to-all-start.1) | async-done | bytes 131104 | tf_op jit(solution)/shard_map/all_to_all | solution.py:484
  48.6 0.6 %reduce_sum.9 = f32[16,128]{1,0:T(8,128)} reduce(f32[16,16,128]{2,1,0:T(8,128)S(1)} %all-to-all-done.1, f32[]{:T(128)} %constant.2.clone.1), dimensions={0}, to_apply=%region_0.0 | reduce | flops 30720 | bytes 139268 | tf_op jit(solution)/shard_map/reduce_sum | solution.py:485
Async XLA Ops:
  0.6 17.4 %copy-start.1 = (f32[1,2,3,16,8,256]{5,4,3,2,1,0:T(8,128)S(1)}, f32[1,2,3,16,8,256]{5,4,3,2,1,0:T(8,128)}, u32[]{:S(2)}) copy-start(f32[1,2,3,16,8,256]{5,4,3,2,1,0:T(8,128)} %param.10) | copy-start | bytes 2359300
  0.6 17.4 %copy-start.2 = (f32[16,8,256]{2,1,0:T(8,128)S(1)}, f32[16,8,256]{2,1,0:T(8,128)}, u32[]{:S(2)}) copy-start(f32[16,8,256]{2,1,0:T(8,128)} %param.8) | copy-start | bytes 393220
  2.8 18.0 %collective-permute-start = (f32[896,128]{1,0:T(8,128)}, f32[896,128]{1,0:T(8,128)S(1)}, u32[]{:S(2)}, u32[]{:S(2)}) collective-permute-start(f32[896,128]{1,0:T(8,128)} %get-tuple-element.12), channel_id=1, source_target_pairs={{0,1},{1,2},{2,3},{3,4},{4,5},{5,6},{6,7},{7,8},{8,9},{9,10},{10,1... | collective-permute-start | bytes 1376264 | tf_op jit(solution)/shard_map/ppermute | solution.py:436
  5.4 15.4 %collective-permute-start.1 = (f32[896,128]{1,0:T(8,128)}, f32[896,128]{1,0:T(8,128)S(1)}, u32[]{:S(2)}, u32[]{:S(2)}) collective-permute-start(f32[896,128]{1,0:T(8,128)} %get-tuple-element.13), channel_id=1, source_target_pairs={{1,0},{2,1},{3,2},{4,3},{5,4},{6,5},{7,6},{8,7},{9,8},{10,9},{11,1... | collective-permute-start | bytes 1376264 | tf_op jit(solution)/shard_map/ppermute | solution.py:437
  10.4 10.4 %copy-start = (f32[1,2,3,16,8,256]{5,4,3,2,1,0:T(8,128)S(1)}, f32[1,2,3,16,8,256]{5,4,3,2,1,0:T(8,128)}, u32[]{:S(2)}) copy-start(f32[1,2,3,16,8,256]{5,4,3,2,1,0:T(8,128)} %param.9) | copy-start | bytes 2359300
  12.1 13.4 %all-to-all-start = ((f32[16,24,128]{2,1,0:T(8,128)}), f32[16,24,128]{2,1,0:T(8,128)S(1)}, u32[]{:S(2)}, u32[]{:S(2)}) async-start(f32[16,24,128]{2,1,0:T(8,128)} %lists.1), calls=%async_computation | async-start | bytes 393216 | tf_op jit(solution)/shard_map/all_to_all | solution.py:438
  30.1 18.5 %all-to-all-start.1 = ((f32[16,16,128]{2,1,0:T(8,128)}), f32[16,16,128]{2,1,0:T(8,128)S(1)}, u32[]{:S(2)}, u32[]{:S(2)}) async-start(f32[16,16,128]{2,1,0:T(8,128)} %bitcast.20), calls=%async_computation.1 | async-start | bytes 262144 | tf_op jit(solution)/shard_map/all_to_all | solution.py:484

commit v5 on v4

--- a/solution.py
+++ b/solution.py
@@ -31,10 +31,15 @@
     return lines.reshape(-1, 2, ROWS, 128).transpose(0, 2, 1, 3).reshape(-1, ROWS, ALONG)
 
 
-def pack_kernel(field_hbm, sigma_hbm, first_hbm, last_hbm, field_ref, sigma_ref, first_ref, last_ref, in_sems, out_sems):
+def pack_kernel(
+    data_hbm, owner_hbm, cell_hbm, field_hbm, sigma_hbm, sent_hbm, first_hbm, last_hbm,
+    data_ref, owner_ref, cell_ref, field_ref, sigma_ref, list_ref, first_ref, last_ref,
+    in_sems, list_sems, out_sems,
+):
     size = LEVELS * WIDE
     block = HALF * 2 * LEVELS
-    pairs = [
+    pairs = [(data_hbm, data_ref), (owner_hbm, owner_ref), (cell_hbm, cell_ref)]
+    pairs += [
         (field_hbm.at[pl.ds(kind * size, size)], field_ref.at[pl.ds(kind * size, size)])
         for kind in range(FIELDS)
     ]
@@ -44,9 +49,22 @@
     ]
     for copy in copies:
         copy.start()
-    sends = []
+    for copy in copies[:3]:
+        copy.wait()
+    for chunk in range(list_ref.shape[0] // 6):
+        lanes = slice(128 * chunk, 128 * chunk + 128)
+        row = 6 * chunk
+        list_ref[row : row + 2] = data_ref[0, :, lanes]
+        list_ref[row + 2 : row + 4] = data_ref[1, :, lanes]
+        list_ref[row + 4 : row + 5] = owner_ref[:, lanes].astype(f32)
+        list_ref[row + 5 : row + 6] = cell_ref[:, lanes].astype(f32)
+    sends = [
+        pltpu.make_async_copy(list_ref, sent_hbm.at[tile], list_sems.at[tile]) for tile in range(sent_hbm.shape[0])
+    ]
+    for copy in sends:
+        copy.start()
     for kind in range(KINDS):
-        copies[kind].wait()
+        copies[3 + kind].wait()
         source, base = (field_ref, kind * LEVELS) if kind < FIELDS else (sigma_ref, 0)
         for x in range(ROWS):
             target = first_ref if x < HALF else last_ref
@@ -60,33 +78,6 @@
             copy = pltpu.make_async_copy(source.at[rows], target.at[rows], out_sems.at[2 * kind + which])
             copy.start()
             sends.append(copy)
-    for copy in sends:
-        copy.wait()
-
-
-def lists_kernel(data_hbm, owner_hbm, cell_hbm, sent_hbm, data_ref, owner_ref, cell_ref, block_ref, in_sems, out_sems):
-    copies = [
-        pltpu.make_async_copy(source, target, in_sems.at[which])
-        for which, (source, target) in enumerate(
-            ((data_hbm, data_ref), (owner_hbm, owner_ref), (cell_hbm, cell_ref))
-        )
-    ]
-    for copy in copies:
-        copy.start()
-    for copy in copies:
-        copy.wait()
-    for chunk in range(block_ref.shape[0] // 6):
-        lanes = slice(128 * chunk, 128 * chunk + 128)
-        row = 6 * chunk
-        block_ref[row : row + 2] = data_ref[0, :, lanes]
-        block_ref[row + 2 : row + 4] = data_ref[1, :, lanes]
-        block_ref[row + 4 : row + 5] = owner_ref[:, lanes].astype(f32)
-        block_ref[row + 5 : row + 6] = cell_ref[:, lanes].astype(f32)
-    sends = [
-        pltpu.make_async_copy(block_ref, sent_hbm.at[tile], out_sems.at[tile]) for tile in range(sent_hbm.shape[0])
-    ]
-    for copy in sends:
-        copy.start()
     for copy in sends:
         copy.wait()
 
@@ -231,7 +222,7 @@
         )
         return carry
 
-    lax.fori_loop(0, sources, step, 0, unroll=8)
+    lax.fori_loop(0, sources, step, 0, unroll=16)
     top = lax.broadcasted_iota(jnp.int32, (8, 128), 0) == 0
     for which in range(4):
         total = acc_ref[32 * which : 32 * which + 16] + acc_ref[32 * which + 16 : 32 * which + 32]
@@ -399,40 +390,37 @@
     smem = pl.BlockSpec(memory_space=pltpu.SMEM)
 
     far = pl.BlockSpec(memory_space=pltpu.HBM)
-    sent = pl.pallas_call(
-        lists_kernel,
-        out_shape=jax.ShapeDtypeStruct((tiles, 6 * listed // 128, 128), f32),
-        in_specs=[far] * 3,
-        out_specs=far,
+    sent, first, last = pl.pallas_call(
+        pack_kernel,
+        out_shape=(
+            jax.ShapeDtypeStruct((tiles, 6 * listed // 128, 128), f32),
+            jax.ShapeDtypeStruct((HALO, 128), f32),
+            jax.ShapeDtypeStruct((HALO, 128), f32),
+        ),
+        in_specs=[far] * 5,
+        out_specs=(far,) * 3,
         scratch_shapes=[
             pltpu.VMEM((2, 2, listed), f32),
             pltpu.VMEM((1, listed), jnp.int32),
             pltpu.VMEM((1, listed), jnp.int32),
+            pltpu.VMEM((LINES, 128), f32),
+            pltpu.VMEM((LEVELS * WIDE, 128), f32),
             pltpu.VMEM((6 * listed // 128, 128), f32),
-            pltpu.SemaphoreType.DMA((3,)),
+            pltpu.VMEM((HALO, 128), f32),
+            pltpu.VMEM((HALO, 128), f32),
+            pltpu.SemaphoreType.DMA((3 + KINDS,)),
             pltpu.SemaphoreType.DMA((tiles,)),
+            pltpu.SemaphoreType.DMA((2 * KINDS,)),
         ],
         cost_estimate=pl.CostEstimate(flops=10**9, bytes_accessed=10**6, transcendentals=0),
-        name="lists",
-    )(station_data.reshape(2, 2, listed), station_owner.reshape(1, listed), station_cell.reshape(1, listed))
-    first, last = pl.pallas_call(
-        pack_kernel,
-        out_shape=(
-            jax.ShapeDtypeStruct((HALO, 128), f32),
-            jax.ShapeDtypeStruct((HALO, 128), f32),
-        ),
-        in_specs=[far] * 2,
-        out_specs=(far, far),
-        scratch_shapes=[
-            pltpu.VMEM((LINES, 128), f32),
-            pltpu.VMEM((LEVELS * WIDE, 128), f32),
-            pltpu.VMEM((HALO, 128), f32),
-            pltpu.VMEM((HALO, 128), f32),
-            pltpu.SemaphoreType.DMA((KINDS,)),
-            pltpu.SemaphoreType.DMA((2 * KINDS,)),
-        ],
         name="pack",
-    )(as_lines(adjoint_start), as_lines(conductivity))
+    )(
+        station_data.reshape(2, 2, listed),
+        station_owner.reshape(1, listed),
+        station_cell.reshape(1, listed),
+        as_lines(adjoint_start),
+        as_lines(conductivity),
+    )
     below = lax.ppermute(last, "tile", [(i, (i + 1) % tiles) for i in range(tiles)])
     above = lax.ppermute(first, "tile", [((i + 1) % tiles, i) for i in range(tiles)])
     got = lax.all_to_all(sent, "tile", 0, 0, tiled=True)

time: 49.5 us -> 49.5 us (level)
  waiting for transfers between devices: 7.43 us -> 10.4 us
  Pallas kernels: 16 us -> 14.3 us
  starting transfers between devices: 23.7 us -> 22.3 us
    ppermute x1, waiting for transfers between devices: 0.69 us -> 2.41 us  [body(): lax.ppermute(last, 'tile', [(i, (i + 1) % tiles) for i in range(tiles)])]
    pallas_call x2 -> x1, Pallas kernels: 3.81 us -> 2.44 us  [body(): pl.pallas_call(pack_kernel, out_shape=(jax.ShapeDtypeStruct((tiles, 6 * l...]
    all_to_all x1, starting transfers between devices: 10.8 us -> 9.42 us  [body(): lax.all_to_all(term.reshape(groups, -1, 128), 'freq', 0, 0, tiled=True)]
    ppermute x1, waiting for transfers between devices: 0.01 us -> 1.3 us  [body(): lax.ppermute(first, 'tile', [((i + 1) % tiles, i) for i in range(tiles)])]
  transfers between devices with their start and end apart: 4 -> 4, of which waited for: 2 -> 3; matrix products, arithmetic and copies ran while one was open for 0% -> 0% of each run, Pallas kernels for 19% -> 15%
where the time goes in v5:
time: 49.5 us; the launch traced here: 49.1 us
  starting transfers between devices  22.3 us (45%)
  Pallas kernels  14.3 us (29%)
  waiting for transfers between devices  10.4 us (21%)
  between operations  1.37 us (3%)
  other arithmetic  0.69 us (1%)
    all_to_all x1, starting transfers between devices, body(): lax.all_to_all(term.reshape(groups, -1, 128), 'freq', 0, 0, tiled=True)  9.42 us
    all_to_all x1, waiting for transfers between devices, body(): lax.all_to_all(term.reshape(groups, -1, 128), 'freq', 0, 0, tiled=True)  6.73 us
    all_to_all x1, starting transfers between devices, body(): got = lax.all_to_all(sent, 'tile', 0, 0, tiled=True)  5.3 us
    ppermute x1, starting transfers between devices, body(): lax.ppermute(first, 'tile', [((i + 1) % tiles, i) for i in range(tiles)])  5.04 us
    pallas_call x1, Pallas kernels, body(): pl.pallas_call(functools.partial(outer_kernel, groups), out_shape=(lines_...  4.69 us
    pallas_call x1, Pallas kernels, body(): pl.pallas_call(functools.partial(source_kernel, groups), out_shape=(lines...  4.3 us
    ppermute x1, starting transfers between devices, body(): lax.ppermute(last, 'tile', [(i, (i + 1) % tiles) for i in range(tiles)])  2.54 us
    pallas_call x1, Pallas kernels, body(): pl.pallas_call(pack_kernel, out_shape=(jax.ShapeDtypeStruct((tiles, 6 * l...  2.44 us
  transfers between devices with their start and end apart: 4, of which 3 were waited for; matrix products, arithmetic and copies ran while one was open for 0% of the time, Pallas kernels for 15%

profile of v5, /device:TPU:1, one launch (start us, length us, event | category | flops | bytes accessed | tf_op | source)
XLA Modules:
  0.0 49.1 jit_solution(6222570671808086360)
XLA Ops:
  0.6 0.0 copy-start.1
  0.6 0.0 copy-start.2
  0.7 0.0 copy-start
  0.7 2.4 %pack.1 = (f32[16,24,128]{2,1,0:T(8,128)}, f32[896,128]{1,0:T(8,128)}, f32[896,128]{1,0:T(8,128)}) custom-call(f32[2,2,512]{2,1,0:T(2,128)} %bitcast.38, s32[1,512]{1,0:T(1,128)} %bitcast.39, s32[1,512]{1,0:T(1,128)} %bitcast.40, f32[1536,128]{1,0:T(8,128)} %bitcast.32, f32[256,128]{1,0:T(8,128)} %bitcast.34), custom_call_target="tpu_custom_call" | custom-call | flops 1000000000 | bytes 1000000 | tf_op jit(solution)/shard_map/pack/pallas_call | solution.py:393
  3.1 2.5 %collective-permute-start = (f32[896,128]{1,0:T(8,128)}, f32[896,128]{1,0:T(8,128)S(1)}, u32[]{:S(2)}, u32[]{:S(2)}) collective-permute-start(f32[896,128]{1,0:T(8,128)} %get-tuple-element.14), channel_id=1, source_target_pairs={{0,1},{1,2},{2,3},{3,4},{4,5},{5,6},{6,7},{7,8},{8,9},{9,10},{10,1... | collective-permute-start | bytes 1376264 | tf_op jit(solution)/shard_map/ppermute | solution.py:424
  5.7 5.0 %collective-permute-start.1 = (f32[896,128]{1,0:T(8,128)}, f32[896,128]{1,0:T(8,128)S(1)}, u32[]{:S(2)}, u32[]{:S(2)}) collective-permute-start(f32[896,128]{1,0:T(8,128)} %get-tuple-element.15), channel_id=1, source_target_pairs={{1,0},{2,1},{3,2},{4,3},{5,4},{6,5},{7,6},{8,7},{9,8},{10,9},{11,1... | collective-permute-start | bytes 1376264 | tf_op jit(solution)/shard_map/ppermute | solution.py:425
  10.7 5.3 %all-to-all-start = ((f32[16,24,128]{2,1,0:T(8,128)}), f32[16,24,128]{2,1,0:T(8,128)S(1)}, u32[]{:S(2)}, u32[]{:S(2)}) async-start(f32[16,24,128]{2,1,0:T(8,128)} %get-tuple-element.13), calls=%async_computation | async-start | bytes 393216 | tf_op jit(solution)/shard_map/all_to_all | solution.py:426
  16.7 0.0 copy-done.1
  16.7 0.0 copy-done.2
  16.7 2.0 %inner.1 = (f32[6,16,2,32,128]{4,3,2,1,0:T(8,128)S(1)}, f32[6,16,2,32,128]{4,3,2,1,0:T(8,128)S(1)}, f32[2,16,2,16,128]{4,3,2,1,0:T(8,128)S(1)}) custom-call(f32[1]{0:T(128)S(6)} %copy.17.omega_ref, f32[1536,128]{1,0:T(8,128)S(1)} %bitcast.33, f32[256,128]{1,0:T(8,128)S(1)} %bitcast.35), custom_call_target="tpu_custom_call" | custom-call | flops 1000000000 | bytes 1000000 | tf_op jit(solution)/shard_map/inner/pallas_call | solution.py:431
  18.6 0.1 pad_add_fusion.place_ref
  18.7 2.4 %collective-permute-done.below_ref = f32[896,128]{1,0:T(8,128)S(1)} collective-permute-done((f32[896,128]{1,0:T(8,128)}, f32[896,128]{1,0:T(8,128)S(1)}, u32[]{:S(2)}, u32[]{:S(2)}) %collective-permute-start) | collective-permute-done | bytes 458784 | tf_op jit(solution)/shard_map/ppermute | solution.py:424
  21.1 1.3 %collective-permute-done.1.above_ref = f32[896,128]{1,0:T(8,128)S(1)} collective-permute-done((f32[896,128]{1,0:T(8,128)}, f32[896,128]{1,0:T(8,128)S(1)}, u32[]{:S(2)}, u32[]{:S(2)}) %collective-permute-start.1) | collective-permute-done | bytes 458784 | tf_op jit(solution)/shard_map/ppermute | solution.py:425
  22.4 0.0 copy-done
  22.4 4.7 %outer.1 = (f32[1536,128]{1,0:T(8,128)S(1)}, f32[256,128]{1,0:T(8,128)S(1)}, f32[6,16,2,32,128]{4,3,2,1,0:T(8,128)S(1)}, f32[6,16,2,32,128]{4,3,2,1,0:T(8,128)S(1)}, f32[2,16,2,16,128]{4,3,2,1,0:T(8,128)S(1)}) custom-call(f32[1]{0:T(128)S(6)} %copy.17.omega_ref, ...), custom_call_target="tpu_custom_call", output_to_operand_aliasing={{2}: (4, {}), {3}: (5, {}), {4}: (6, {})} | custom-call | flops 1000000000 | bytes 1000000 | tf_op jit(solution)/shard_map/outer/pallas_call | solution.py:444
  27.1 0.0 all-to-all-done.lists_ref
  27.1 4.3 %source.1 = (f32[1536,128]{1,0:T(8,128)S(1)}, f32[256,128]{1,0:T(8,128)}) custom-call(f32[1]{0:T(128)S(6)} %copy.17.omega_ref, s32[2]{0:T(128)S(1)} %pad_add_fusion.place_ref, f32[16,24,128]{2,1,0:T(8,128)S(1)} %all-to-all-done.lists_ref, f32[2,16,2,16,128]{4,3,2,1,0:T(8,128)S(1)} %get-tuple-element.19.coef, ...), custom_call_target="tpu_custom_call", output_to_operand_aliasing={{0}: (5, {})} | custom-call | flops 1000000000 | bytes 1000000 | tf_op jit(solution)/shard_map/source/pallas_call | solution.py:455
  31.4 9.4 %all-to-all-start.1 = ((f32[16,16,128]{2,1,0:T(8,128)}), f32[16,16,128]{2,1,0:T(8,128)S(1)}, u32[]{:S(2)}, u32[]{:S(2)}) async-start(f32[16,16,128]{2,1,0:T(8,128)} %bitcast.20), calls=%async_computation.1 | async-start | bytes 262144 | tf_op jit(solution)/shard_map/all_to_all | solution.py:472
  40.9 0.9 %store.1 = f32[1536,128]{1,0:T(8,128)} custom-call(f32[1536,128]{1,0:T(8,128)S(1)} %get-tuple-element.22.value_ref), custom_call_target="tpu_custom_call" | custom-call | tf_op jit(solution)/shard_map/store/pallas_call | solution.py:474
  41.8 6.7 %all-to-all-done.1 = f32[16,16,128]{2,1,0:T(8,128)S(1)} async-done(((f32[16,16,128]{2,1,0:T(8,128)}), f32[16,16,128]{2,1,0:T(8,128)S(1)}, u32[]{:S(2)}, u32[]{:S(2)}) %all-to-all-start.1) | async-done | bytes 131104 | tf_op jit(solution)/shard_map/all_to_all | solution.py:472
  48.5 0.6 %reduce_sum.9 = f32[16,128]{1,0:T(8,128)} reduce(f32[16,16,128]{2,1,0:T(8,128)S(1)} %all-to-all-done.1, f32[]{:T(128)} %constant.2.clone.1), dimensions={0}, to_apply=%region_0.0 | reduce | flops 30720 | bytes 139268 | tf_op jit(solution)/shard_map/reduce_sum | solution.py:473
Async XLA Ops:
  0.6 16.0 %copy-start.1 = (f32[1,2,3,16,8,256]{5,4,3,2,1,0:T(8,128)S(1)}, f32[1,2,3,16,8,256]{5,4,3,2,1,0:T(8,128)}, u32[]{:S(2)}) copy-start(f32[1,2,3,16,8,256]{5,4,3,2,1,0:T(8,128)} %param.10) | copy-start | bytes 2359300
  0.6 16.0 %copy-start.2 = (f32[16,8,256]{2,1,0:T(8,128)S(1)}, f32[16,8,256]{2,1,0:T(8,128)}, u32[]{:S(2)}) copy-start(f32[16,8,256]{2,1,0:T(8,128)} %param.8) | copy-start | bytes 393220
  0.7 21.8 %copy-start = (f32[1,2,3,16,8,256]{5,4,3,2,1,0:T(8,128)S(1)}, f32[1,2,3,16,8,256]{5,4,3,2,1,0:T(8,128)}, u32[]{:S(2)}) copy-start(f32[1,2,3,16,8,256]{5,4,3,2,1,0:T(8,128)} %param.9) | copy-start | bytes 2359300
  3.1 18.0 %collective-permute-start = (f32[896,128]{1,0:T(8,128)}, f32[896,128]{1,0:T(8,128)S(1)}, u32[]{:S(2)}, u32[]{:S(2)}) collective-permute-start(f32[896,128]{1,0:T(8,128)} %get-tuple-element.14), channel_id=1, source_target_pairs={{0,1},{1,2},{2,3},{3,4},{4,5},{5,6},{6,7},{7,8},{8,9},{9,10},{10,1... | collective-permute-start | bytes 1376264 | tf_op jit(solution)/shard_map/ppermute | solution.py:424
  5.7 16.8 %collective-permute-start.1 = (f32[896,128]{1,0:T(8,128)}, f32[896,128]{1,0:T(8,128)S(1)}, u32[]{:S(2)}, u32[]{:S(2)}) collective-permute-start(f32[896,128]{1,0:T(8,128)} %get-tuple-element.15), channel_id=1, source_target_pairs={{1,0},{2,1},{3,2},{4,3},{5,4},{6,5},{7,6},{8,7},{9,8},{10,9},{11,1... | collective-permute-start | bytes 1376264 | tf_op jit(solution)/shard_map/ppermute | solution.py:425
  10.7 16.4 %all-to-all-start = ((f32[16,24,128]{2,1,0:T(8,128)}), f32[16,24,128]{2,1,0:T(8,128)S(1)}, u32[]{:S(2)}, u32[]{:S(2)}) async-start(f32[16,24,128]{2,1,0:T(8,128)} %get-tuple-element.13), calls=%async_computation | async-start | bytes 393216 | tf_op jit(solution)/shard_map/all_to_all | solution.py:426
  31.4 17.1 %all-to-all-start.1 = ((f32[16,16,128]{2,1,0:T(8,128)}), f32[16,16,128]{2,1,0:T(8,128)S(1)}, u32[]{:S(2)}, u32[]{:S(2)}) async-start(f32[16,16,128]{2,1,0:T(8,128)} %bitcast.20), calls=%async_computation.1 | async-start | bytes 262144 | tf_op jit(solution)/shard_map/all_to_all | solution.py:472
